TPU v7x, 32 devices: a whole 2x2x4 slice. The times are simulated.
32 devices in a mesh: seq: 8 (over z, y), rep: 4 (over x, core).
Axes of the slice: x: 2, y: 2, z: 4, core: 2. Of those that a mesh axis runs over, the one named last changes fastest.
Arguments:
- reference_acts: bfloat16 [2048, 1536], P('seq'), may hold values from -6 to 6
- owners: int32 [128, 1], P('seq'), may hold values from 0 to 7; in each aligned block of 16 rows (0 to 15, 16 to 31, ...) at most 4 rows name the same one
- offsets: int32 [128], P('seq'), may hold values from 0 to 255
- codes: int32 [128], P('seq'), may hold values from 0 to 3
- base_delta: bfloat16 [4, 1536], replicated, may hold values from -6 to 6
- gain_one: bfloat16 [1536], replicated, may hold values from 0.25 to 1.75
- conv_one: bfloat16 [3, 1536, 768], replicated, may hold values from -0.09375 to 0.09375
- proj_one: bfloat16 [768, 1536], replicated, may hold values from -0.21875 to 0.21875
- gain_two: bfloat16 [1536], replicated, may hold values from 0.25 to 1.75
- conv_two: bfloat16 [3, 1536, 768], replicated, may hold values from -0.09375 to 0.09375
- proj_two: bfloat16 [768, 1536], replicated, may hold values from -0.21875 to 0.21875
- head_weight: bfloat16 [1536, 4096], P(None, 'rep'), may hold values from -0.15625 to 0.15625
- head_bias: bfloat16 [4096], P('rep'), may hold values from -1 to 1
Outputs:
- scores: float32 [128, 4096], P('seq', 'rep')
Inputs may be any that keep to these rules, and one draw needn't show every extreme that they name: `owners`: no window is named by more than 4 variants of the list of one index of seq, a bound that some block reaches.
All inputs are finite; a program needn't handle non-finite values.
Results may differ from a plain program's by a relative error of at most 0.017.
Values may be sent and summed in bfloat16 or wider, within the bound.
No kernel may reach another device: no remote copies, remote signals or barrier semaphores. Data moves between devices by JAX's collectives and lax.ppermute only.
A program may use at most 128 MiB of HBM per device.

v0:
```python
import functools

import jax
import jax.numpy as jnp
from jax import lax
from jax.experimental import pallas as pl
from jax.experimental.pallas import tpu as pltpu
from jax.sharding import PartitionSpec as P

D1 = 8
D2 = 64
REACH = 2 * (D1 + D2)
EPS = 1e-05
NT = 256
F32 = jnp.float32
BF16 = jnp.bfloat16


def gelu(x):
    inner = 0.7978845608028654 * (x + 0.044715 * (x * x * x))
    return x * (0.5 * (1.0 + jnp.tanh(inner)))


def softplus(x):
    return jnp.maximum(x, 0.0) + jnp.log1p(jnp.exp(-jnp.abs(x)))


def trunk_kernel(
    slots,
    half_cap,
    genome,
    desc_ref,
    acts_ref,
    halo_ref,
    pair_ref,
    delta_ref,
    gain1_ref,
    gain2_ref,
    bias_ref,
    pair_bias_ref,
    conv1_ref,
    proj1_ref,
    conv2_ref,
    proj2_ref,
    head_ref,
    pair_head_ref,
    out_ref,
    xp,
    w1,
    p1,
    w2,
    p2,
    hw,
    fields,
    xg,
    xalt,
    n1,
    g,
    h1,
    n2,
    h2,
    delta_v,
    gain1_v,
    gain2_v,
    bias_v,
    pair_bias_v,
    sem,
):
    S = slots
    lists = desc_ref.shape[0]
    width, C = acts_ref.shape
    half = p1.shape[0]
    tracks = head_ref.shape[1]
    here = lax.axis_index("seq")
    core = lax.rem(lax.axis_index("rep"), 2)
    other = 1 - core

    def rows(start):
        return pl.ds(pl.multiple_of(start, 16), REACH)

    copies = [
        (acts_ref, xp.at[pl.ds(REACH, width)]),
        (halo_ref, xp.at[rows(core * (REACH + width))]),
        (pair_ref, xp.at[rows(other * (REACH + width))]),
        (conv1_ref.at[0], w1.at[0]),
        (conv1_ref.at[1], w1.at[1]),
        (conv1_ref.at[2], w1.at[2]),
        (proj1_ref, p1),
        (conv2_ref.at[0], w2.at[0]),
        (conv2_ref.at[1], w2.at[1]),
        (conv2_ref.at[2], w2.at[2]),
        (proj2_ref, p2),
        (head_ref, hw.at[core]),
        (pair_head_ref, hw.at[other]),
        (delta_ref, delta_v),
        (gain1_ref, gain1_v),
        (gain2_ref, gain2_v),
        (bias_ref, bias_v),
        (pair_bias_ref, pair_bias_v),
    ]
    copies = [pltpu.make_async_copy(a, b, sem.at[i]) for i, (a, b) in enumerate(copies)]
    for copy in copies[13:] + copies[:13]:
        copy.start()

    for s in range(lists):
        for f in range(3):
            fields[f, s * half_cap : (s + 1) * half_cap, :] = jnp.broadcast_to(
                desc_ref[s, f : f + 1, :], (half_cap, 128)
            )
    hit = fields[0] == here
    upper = (
        lax.broadcasted_iota(jnp.int32, (128, 128), 0)
        < lax.broadcasted_iota(jnp.int32, (128, 128), 1)
    )
    rank = jnp.dot(
        jnp.where(hit, 1.0, 0.0).astype(BF16),
        jnp.where(upper, 1.0, 0.0).astype(BF16),
        preferred_element_type=F32,
    )
    want = core * half_cap + lax.rem(lax.broadcasted_iota(jnp.int32, (S, 128), 0), half_cap)
    chosen = hit & (rank == want.astype(F32))
    offset = jnp.sum(jnp.where(chosen, fields[1].astype(F32), 0.0), axis=1, keepdims=True)
    offset = offset.astype(jnp.int32)
    code = jnp.sum(jnp.where(chosen, fields[2].astype(F32), 0.0), axis=1, keepdims=True)
    where_bin = here * width + offset

    def inside(j, m):
        at = where_bin + (j * D1 + m * D2)
        return (at >= 0) & (at < genome)

    span = 2 * width
    low = 2 * (D1 + D2) * 2 + width - span
    column = lax.broadcasted_iota(jnp.int32, (S, span), 1)

    def pick(a, m, base):
        return jnp.where(column == offset + (a * D1 + m * D2 - base), 1.0, 0.0).astype(BF16)

    early = jnp.concatenate([pick(a, m, 0) for a in range(5) for m in range(4)], axis=0)
    late = jnp.concatenate([pick(a, 4, low) for a in range(5)], axis=0)
    for copy in copies[13:] + copies[:3]:
        copy.wait()
    for n in range(C // NT):
        at = pl.ds(n * NT, NT)
        first = jnp.dot(early, xp[:span, at], preferred_element_type=F32).astype(BF16)
        last = jnp.dot(late, xp[low : low + span, at], preferred_element_type=F32).astype(BF16)
        for a in range(5):
            xg[a * 5 * S : (a * 5 + 4) * S, at] = first[a * 4 * S : (a + 1) * 4 * S]
            xg[(a * 5 + 4) * S : (a * 5 + 5) * S, at] = last[a * S : (a + 1) * S]
    bump = jnp.zeros((S, C), F32)
    for k in range(4):
        bump = jnp.where(code == k, delta_v[k : k + 1, :].astype(F32), bump)
    xalt[...] = xg[12 * S : 13 * S, :].astype(F32) + bump

    def normed(values, gain):
        scale = lax.rsqrt(jnp.mean(values * values, axis=-1, keepdims=True) + EPS)
        return (values * scale * gain).astype(BF16)

    gain1 = gain1_v[...].astype(F32).reshape(1, C)
    for b in range(25):
        n1[b * S : (b + 1) * S, :] = normed(xg[b * S : (b + 1) * S, :].astype(F32), gain1)
    n1[25 * S : 26 * S, :] = normed(xalt[...], gain1)

    for copy in copies[3:6]:
        copy.wait()
    for n in range(half // NT):
        at = pl.ds(n * NT, NT)
        taps = []
        for k in range(3):
            left = jnp.concatenate(
                [n1[k * 5 * S : (k + 3) * 5 * S, :], n1[25 * S : 26 * S, :]], axis=0
            )
            taps.append(jnp.dot(left, w1[k, :, at], preferred_element_type=F32))
        total = (taps[0] + taps[1]) + taps[2]
        g[: 15 * S, at] = gelu(total[: 15 * S]).astype(BF16)
        for j in range(3):
            base = (j * 5 + 2) * S
            parts = [
                taps[k][15 * S : 16 * S] if k == 2 - j else taps[k][base : base + S]
                for k in range(3)
            ]
            g[(15 + j) * S : (16 + j) * S, at] = gelu((parts[0] + parts[1]) + parts[2]).astype(BF16)

    copies[6].wait()
    for n in range(C // NT):
        at = pl.ds(n * NT, NT)
        delta = jnp.dot(g[...], p1[:, at], preferred_element_type=F32)
        for j in range(3):
            for m in range(5):
                b = j * 5 + m
                x = xg[(b + 5) * S : (b + 6) * S, at].astype(F32)
                h = jnp.where(inside(j - 1, m - 2), x + delta[b * S : (b + 1) * S], 0.0)
                h1[(m * 3 + j) * S : (m * 3 + j + 1) * S, at] = h.astype(BF16)
            b = 15 + j
            x = xalt[:, at] if j == 1 else xg[(j * 5 + 7) * S : (j * 5 + 8) * S, at].astype(F32)
            h = jnp.where(inside(j - 1, 0), x + delta[b * S : (b + 1) * S], 0.0)
            h1[b * S : (b + 1) * S, at] = h.astype(BF16)
    gain2 = gain2_v[...].astype(F32).reshape(1, C)
    for b in range(18):
        n2[b * S : (b + 1) * S, :] = normed(h1[b * S : (b + 1) * S, :].astype(F32), gain2)

    for copy in copies[7:10]:
        copy.wait()
    for n in range(half // NT):
        at = pl.ds(n * NT, NT)
        taps = []
        for k in range(3):
            left = jnp.concatenate(
                [n2[k * 3 * S : (k + 3) * 3 * S, :], n2[15 * S : 18 * S, :]], axis=0
            )
            taps.append(jnp.dot(left, w2[k, :, at], preferred_element_type=F32))
        total = (taps[0] + taps[1]) + taps[2]
        g[: 9 * S, at] = gelu(total[: 9 * S]).astype(BF16)
        for i in range(3):
            base = i * 3 * S
            parts = [
                taps[k][9 * S : 12 * S] if k == 2 - i else taps[k][base : base + 3 * S]
                for k in range(3)
            ]
            g[(9 + 3 * i) * S : (12 + 3 * i) * S, at] = gelu(
                (parts[0] + parts[1]) + parts[2]
            ).astype(BF16)

    copies[10].wait()
    for n in range(C // NT):
        at = pl.ds(n * NT, NT)
        delta = jnp.dot(g[...], p2[:, at], preferred_element_type=F32)
        for i in range(3):
            plain = h1[(i + 1) * 3 * S : (i + 2) * 3 * S, at].astype(F32)
            changed = h1[15 * S : 18 * S, at].astype(F32) if i == 1 else plain
            lo = i * 3 * S
            h2[lo : lo + 3 * S, at] = (plain + delta[lo : lo + 3 * S]).astype(BF16)
            lo += 9 * S
            h2[lo : lo + 3 * S, at] = (changed + delta[lo : lo + 3 * S]).astype(BF16)

    for copy in copies[11:13]:
        copy.wait()
    keep = [
        jnp.where(inside(j - 1, i - 1), 1.0, 0.0) for i in range(3) for j in range(3)
    ]
    for side in range(2):
        bias = jnp.where(core == side, bias_v[...].astype(F32), pair_bias_v[...].astype(F32)).reshape(1, tracks)
        for n in range(tracks // NT):
            at = pl.ds(n * NT, NT)
            logits = jnp.dot(h2[...], hw[side, :, at], preferred_element_type=F32)
            cover = softplus(logits + bias[:, n * NT : (n + 1) * NT])
            score = jnp.zeros((S, NT), F32)
            for b in range(9):
                change = cover[(9 + b) * S : (10 + b) * S] - cover[b * S : (b + 1) * S]
                score = score + change * keep[b]
            per = tracks // 128
            for t in range(NT // 128):
                start = side * S * per + n * (NT // 128) + t
                out_ref[pl.ds(start, S, stride=per), :] = score[:, t * 128 : (t + 1) * 128]


def trunk_and_head(desc, acts, halo, pair, delta, gain1, gain2, bias, pair_bias, weights, genome, half_cap):
    conv1, proj1, conv2, proj2, head, pair_head = weights
    lists = desc.shape[0]
    S = lists * half_cap
    width, C = acts.shape
    half = proj1.shape[0]
    tracks = head.shape[1]
    vm = pl.BlockSpec(memory_space=pltpu.VMEM)
    hbm = pl.BlockSpec(memory_space=pltpu.HBM)
    free = pl.BlockSpec(memory_space=pl.ANY)
    macs = S * (48 * C * half + 18 * C * half + 36 * C * half + 18 * C * half + 36 * C * tracks)
    acts, delta, gain1, gain2, bias, conv1, proj1, conv2, proj2, head = (
        pltpu.with_memory_space_constraint(a, pltpu.HBM)
        for a in (acts, delta, gain1, gain2, bias, conv1, proj1, conv2, proj2, head)
    )
    return pl.pallas_call(
        functools.partial(trunk_kernel, S, half_cap, genome),
        out_shape=jax.ShapeDtypeStruct((2 * S * tracks // 128, 128), F32),
        in_specs=[vm, hbm, free, free] + [hbm] * 4 + [free] + [hbm] * 5 + [free],
        out_specs=vm,
        scratch_shapes=[
            pltpu.VMEM((width + 2 * REACH, C), BF16),
            pltpu.VMEM((3, C, half), BF16),
            pltpu.VMEM((half, C), BF16),
            pltpu.VMEM((3, C, half), BF16),
            pltpu.VMEM((half, C), BF16),
            pltpu.VMEM((2, C, tracks), BF16),
            pltpu.VMEM((3, S, 128), jnp.int32),
            pltpu.VMEM((25 * S, C), BF16),
            pltpu.VMEM((S, C), F32),
            pltpu.VMEM((26 * S, C), BF16),
            pltpu.VMEM((18 * S, half), BF16),
            pltpu.VMEM((18 * S, C), BF16),
            pltpu.VMEM((18 * S, C), BF16),
            pltpu.VMEM((18 * S, C), BF16),
            pltpu.VMEM(delta.shape, BF16),
            pltpu.VMEM(gain1.shape, BF16),
            pltpu.VMEM(gain2.shape, BF16),
            pltpu.VMEM(bias.shape, BF16),
            pltpu.VMEM(bias.shape, BF16),
            pltpu.SemaphoreType.DMA((18,)),
        ],
        compiler_params=pltpu.CompilerParams(vmem_limit_bytes=36 * 1024 * 1024),
        cost_estimate=pl.CostEstimate(
            flops=2 * macs, bytes_accessed=28 * 1024 * 1024, transcendentals=S * 18 * (half * 2 + tracks * 4)
        ),
        name="trunk_and_head",
    )(desc, acts, halo, pair, delta, gain1, gain2, bias, pair_bias, conv1, proj1, conv2, proj2, head, pair_head)


def return_kernel(n_seq, half_cap, owners_ref, got_ref, out_ref, tiles):
    count, tracks = out_ref.shape
    per = tracks // 128
    for v in range(count):
        mine = owners_ref[v]
        rank = jnp.int32(0)
        for u in range(v):
            rank = rank + jnp.where(owners_ref[u] == mine, 1, 0)
        side = lax.div(rank, half_cap)
        row = ((side * n_seq + mine) * half_cap + (rank - side * half_cap)) * per
        tiles[v * per : (v + 1) * per, :] = got_ref[pl.ds(pl.multiple_of(row, 8), per), :]
    for t in range(per):
        out_ref[:, t * 128 : (t + 1) * 128] = tiles[pl.ds(t, count, stride=per), :]


def per_device(
    reference_acts,
    owners,
    offsets,
    codes,
    base_delta,
    gain_one,
    conv_one,
    proj_one,
    gain_two,
    conv_two,
    proj_two,
    head_weight,
    head_bias,
):
    n_seq = lax.axis_size("seq")
    n_rep = lax.axis_size("rep")
    width = reference_acts.shape[0]
    genome = width * n_seq
    core = lax.axis_index("rep") % 2
    vcount = owners.shape[0]
    half_cap = max(2, 2 * vcount // n_seq) // 2
    tracks = head_weight.shape[1]
    swap = [(r, r ^ 1) for r in range(n_rep)]
    steps = [(i, r, i + 1 - 2 * (r % 2)) for i in range(n_seq) for r in range(n_rep)]
    edges = [(i * n_rep + r, j * n_rep + r) for i, r, j in steps if 0 <= j < n_seq]

    owner = owners[:, 0]
    fields = jnp.stack([owner, offsets, codes])
    fields = jnp.pad(fields, ((0, 5), (0, 128 - vcount)), constant_values=-1)
    edge = lax.dynamic_slice_in_dim(reference_acts, (1 - core) * (width - REACH), REACH, 0)
    halo = lax.ppermute(edge, ("seq", "rep"), edges)
    pair_head = lax.ppermute(head_weight, "rep", swap)
    pair_bias = lax.ppermute(head_bias, "rep", swap)
    desc = lax.all_to_all(
        jnp.broadcast_to(fields[None], (n_seq, 8, 128)), "seq", split_axis=0, concat_axis=0, tiled=True
    )
    halo, desc = lax.optimization_barrier((halo, desc))
    pair = lax.ppermute(halo, "rep", swap)
    scores = trunk_and_head(
        desc,
        reference_acts,
        halo,
        pair,
        base_delta,
        gain_one,
        gain_two,
        head_bias,
        pair_bias,
        (conv_one, proj_one, conv_two, proj_two, head_weight, pair_head),
        genome,
        half_cap,
    )
    per = tracks // 128
    groups = [
        [s * n_rep + x + c for c in range(2) for s in range(n_seq)] for x in range(0, n_rep, 2)
    ]
    got = lax.all_to_all(
        scores.reshape(2 * n_seq, half_cap * per, 128),
        ("seq", "rep"),
        split_axis=0,
        concat_axis=0,
        axis_index_groups=groups,
        tiled=True,
    ).reshape(2 * n_seq * half_cap * per, 128)
    return pl.pallas_call(
        functools.partial(return_kernel, n_seq, half_cap),
        out_shape=jax.ShapeDtypeStruct((vcount, tracks), F32),
        in_specs=[pl.BlockSpec(memory_space=pltpu.SMEM), pl.BlockSpec(memory_space=pltpu.VMEM)],
        out_specs=pl.BlockSpec(memory_space=pltpu.VMEM),
        scratch_shapes=[pltpu.VMEM((vcount * per, 128), F32)],
        name="pick_scores",
    )(owner, got)


def solution(mesh):
    return jax.shard_map(
        per_device,
        mesh=mesh,
        in_specs=(
            P("seq", None),
            P("seq", None),
            P("seq"),
            P("seq"),
            P(),
            P(),
            P(),
            P(),
            P(),
            P(),
            P(),
            P(None, "rep"),
            P("rep"),
        ),
        out_specs=P("seq", "rep"),
        check_vma=False,
    )
```

profile of v0, /device:TPU:0, one launch (start us, length us, event | category | flops | bytes accessed | tf_op | source)
XLA Modules:
  0.0 47.7 jit_solution(6253309390632083136)
XLA Ops:
  0.0 0.5 collective-permute-start.3
  0.5 1.0 %constant_dynamic-slice_fusion = bf16[144,1536]{1,0:T(8,128)(2,1)S(1)} fusion(bf16[256,1536]{1,0:T(8,128)(2,1)} %acts_ref.1, s32[]{:T(128)S(6)} %select_n.11), kind=kLoop, calls=%fused_computation.1 | loop fusion | bytes 884740 | tf_op jit(solution)/shard_map/dynamic_slice | solution.py:351
  1.5 4.4 %collective-permute-start = (bf16[144,1536]{1,0:T(8,128)(2,1)S(1)}, bf16[144,1536]{1,0:T(8,128)(2,1)S(1)}, u32[]{:S(2)}, u32[]{:S(2)}) collective-permute-start(bf16[144,1536]{1,0:T(8,128)(2,1)S(1)} %constant_dynamic-slice_fusion), channel_id=1, source_target_pairs={{0,4},{2,6},{4,8},{5,1},{6,10},{7,3},{8,12},{9,5},{10,14},{11,7},{... | collective-permute-start | bytes 1327112 | tf_op jit(solution)/shard_map/ppermute | solution.py:352
  6.0 0.7 %pad_add_fusion = s32[3,16]{1,0:T(4,128)S(1)} fusion(s32[1,16]{1,0:T(1,128)} %bitcast.10, s32[1,16]{1,0:T(1,128)} %bitcast.11, s32[1,16]{1,0:T(1,128)} %bitcast.8), kind=kLoop, calls=%fused_computation | loop fusion | flops 96 | bytes 384 | tf_op jit(solution)/shard_map/stack | solution.py:349
  6.7 11.3 %all_to_all.10.desc_ref = s32[8,8,128]{2,1,0:T(8,128)S(1)} all-to-all(s32[8,8,128]{2,1,0:T(8,128)S(1)} %broadcast_in_dim.2), channel_id=1, replica_groups=mesh['seq'=8,'rep'=4] {'seq'}, dimensions={0} | all-to-all | bytes 65536 | tf_op jit(solution)/shard_map/all_to_all | solution.py:355
  18.0 0.0 collective-permute-done.halo_ref
  18.0 0.0 collective-permute-start.1
  18.0 0.5 %collective-permute-start.2 = (bf16[1024]{0:T(1024)(128)(2,1)}, bf16[1024]{0:T(1024)(128)(2,1)S(1)}, u32[]{:S(2)}, u32[]{:S(2)}) collective-permute-start(bf16[1024]{0:T(1024)(128)(2,1)} %bias_ref.1), channel_id=1, source_target_pairs={{0,1},{1,0},{2,3},{3,2},{4,5},{5,4},{6,7},{7,6},{8,9},{9,8},{10,11... | collective-permute-start | bytes 6152 | tf_op jit(solution)/shard_map/ppermute | solution.py:354
  18.5 1.1 %collective-permute-done.2.pair_bias_ref = bf16[1024]{0:T(1024)(128)(2,1)S(1)} collective-permute-done((bf16[1024]{0:T(1024)(128)(2,1)}, bf16[1024]{0:T(1024)(128)(2,1)S(1)}, u32[]{:S(2)}, u32[]{:S(2)}) %collective-permute-start.2) | collective-permute-done | bytes 2080 | tf_op jit(solution)/shard_map/ppermute | solution.py:354
  19.7 0.2 collective-permute-done.1.pair_ref
  19.8 0.0 collective-permute-done.3.pair_head_ref
  19.8 13.9 %trunk_and_head.1 = f32[256,128]{1,0:T(8,128)S(1)} custom-call(s32[8,8,128]{2,1,0:T(8,128)S(1)} %all_to_all.10.desc_ref, bf16[256,1536]{1,0:T(8,128)(2,1)} %acts_ref.1, bf16[144,1536]{1,0:T(8,128)(2,1)S(1)} %collective-permute-done.halo_ref, bf16[144,1536]{1,0:T(8,128)(2,1)S(1)} %collective-permute-done.1.pair_ref, bf16[4,1536]{1,0:T(4,128)(2,1)} %delta_ref.1, ...), custom_call_target="tpu_custom_call" | custom-call | flops 6341787648 | bytes 29360128 | tf_op jit(solution)/shard_map/trunk_and_head/pallas_call | solution.py:271
  33.7 12.3 %all_to_all.11 = f32[16,16,128]{2,1,0:T(8,128)} all-to-all(f32[16,16,128]{2,1,0:T(8,128)S(1)} %bitcast.6), channel_id=1, replica_groups={{0,4,8,12,16,20,24,28,1,5,9,13,17,21,25,29},{2,6,10,14,18,22,26,30,3,7,..., dimensions={0} | all-to-all | bytes 262144 | tf_op jit(solution)/shard_map/all_to_all | solution.py:378
  46.0 1.7 %pick_scores.1 = f32[16,1024]{1,0:T(8,128)} custom-call(s32[16]{0:T(128)} %bitcast.9, f32[256,128]{1,0:T(8,128)} %bitcast.7), custom_call_target="tpu_custom_call" | custom-call | tf_op jit(solution)/shard_map/pick_scores/pallas_call | solution.py:386
  (2 shorter events, 0.0 us)
Async XLA Ops:
  0.0 19.8 %collective-permute-start.3 = (bf16[1536,1024]{1,0:T(8,128)(2,1)}, bf16[1536,1024]{1,0:T(8,128)(2,1)S(1)}, u32[]{:S(2)}, u32[]{:S(2)}) collective-permute-start(bf16[1536,1024]{1,0:T(8,128)(2,1)} %head_ref.1), channel_id=1, source_target_pairs={{0,1},{1,0},{2,3},{3,2},{4,5},{5,4},{6,7},{7,6},{8,9},{9,8},{10,11... | collective-permute-start | bytes 9437192 | tf_op jit(solution)/shard_map/ppermute | solution.py:353
  1.5 16.5 %collective-permute-start = (bf16[144,1536]{1,0:T(8,128)(2,1)S(1)}, bf16[144,1536]{1,0:T(8,128)(2,1)S(1)}, u32[]{:S(2)}, u32[]{:S(2)}) collective-permute-start(bf16[144,1536]{1,0:T(8,128)(2,1)S(1)} %constant_dynamic-slice_fusion), channel_id=1, source_target_pairs={{0,4},{2,6},{4,8},{5,1},{6,10},{7,3},{8,12},{9,5},{10,14},{11,7},{... | collective-permute-start | bytes 1327112 | tf_op jit(solution)/shard_map/ppermute | solution.py:352
  18.0 1.8 %collective-permute-start.1 = (bf16[144,1536]{1,0:T(8,128)(2,1)S(1)}, bf16[144,1536]{1,0:T(8,128)(2,1)S(1)}, u32[]{:S(2)}, u32[]{:S(2)}) collective-permute-start(bf16[144,1536]{1,0:T(8,128)(2,1)S(1)} %collective-permute-done.halo_ref), channel_id=1, source_target_pairs={{0,1},{1,0},{2,3},{3,2},{4,5},{5,4},{6,7},{7,6},{8,9},{9,8},{10,11... | collective-permute-start | bytes 1327112 | tf_op jit(solution)/shard_map/ppermute | solution.py:359
  18.0 1.6 %collective-permute-start.2 = (bf16[1024]{0:T(1024)(128)(2,1)}, bf16[1024]{0:T(1024)(128)(2,1)S(1)}, u32[]{:S(2)}, u32[]{:S(2)}) collective-permute-start(bf16[1024]{0:T(1024)(128)(2,1)} %bias_ref.1), channel_id=1, source_target_pairs={{0,1},{1,0},{2,3},{3,2},{4,5},{5,4},{6,7},{7,6},{8,9},{9,8},{10,11... | collective-permute-start | bytes 6152 | tf_op jit(solution)/shard_map/ppermute | solution.py:354
where the time goes:
time: 48 us; the launch traced here: 47.7 us
  blocking collectives  23.6 us (49%)
  Pallas kernels  15.6 us (32%)
  starting transfers between devices  5.41 us (11%)
  waiting for transfers between devices  1.29 us (3%)
  local copies, waits for them, and re-layouts  1.06 us (2%)
  other arithmetic  0.7 us (1%)
    pallas_call x1, Pallas kernels, trunk_and_head(): pl.pallas_call(functools.partial(trunk_kernel, S, half_cap, genome), out_...  13.9 us
    all_to_all x1, blocking collectives, per_device(): lax.all_to_all(scores.reshape(2 * n_seq, half_cap * per, 128), ('seq', 'r...  12.3 us
    all_to_all x1, blocking collectives, per_device(): lax.all_to_all(jnp.broadcast_to(fields[None], (n_seq, 8, 128)), 'seq', sp...  11.3 us
    ppermute x1, starting transfers between devices, per_device(): halo = lax.ppermute(edge, ('seq', 'rep'), edges)  4.45 us
    pallas_call x1, Pallas kernels, per_device(): pl.pallas_call(functools.partial(return_kernel, n_seq, half_cap), out_sha...  1.74 us
    ppermute x1, waiting for transfers between devices, per_device(): pair_bias = lax.ppermute(head_bias, 'rep', swap)  1.13 us
    dynamic_slice x1, local copies, waits for them, and re-layouts, per_device(): lax.dynamic_slice_in_dim(reference_acts, (1 - core) * (width - REACH), RE...  1.04 us
  transfers between devices with their start and end apart: 4, of which 2 were waited for; matrix products, arithmetic and copies ran while one was open for 4% of the time, Pallas kernels for 0%

commit v1 on v0

v1 whole, which is shorter than its diff:
```python
import functools

import jax
import jax.numpy as jnp
from jax import lax
from jax.experimental import pallas as pl
from jax.experimental.pallas import tpu as pltpu
from jax.sharding import PartitionSpec as P

D1 = 8
D2 = 64
REACH = 2 * (D1 + D2)
EPS = 1e-05
NT = 256
F32 = jnp.float32
BF16 = jnp.bfloat16


def gelu(x):
    inner = 0.7978845608028654 * (x + 0.044715 * (x * x * x))
    return x * (0.5 * (1.0 + jnp.tanh(inner)))


def softplus(x):
    return jnp.maximum(x, 0.0) + jnp.log1p(jnp.exp(-jnp.abs(x)))


def slot_kernel(half_cap, desc_ref, slots_ref, fields):
    lists = desc_ref.shape[0]
    S = lists * half_cap
    here = lax.axis_index("seq")
    core = lax.rem(lax.axis_index("rep"), 2)
    for s in range(lists):
        for f in range(3):
            fields[f, s * half_cap : (s + 1) * half_cap, :] = jnp.broadcast_to(
                desc_ref[s, f : f + 1, :], (half_cap, 128)
            )
    hit = fields[0] == here
    upper = (
        lax.broadcasted_iota(jnp.int32, (128, 128), 0)
        < lax.broadcasted_iota(jnp.int32, (128, 128), 1)
    )
    rank = jnp.dot(
        jnp.where(hit, 1.0, 0.0).astype(BF16),
        jnp.where(upper, 1.0, 0.0).astype(BF16),
        preferred_element_type=F32,
    )
    want = core * half_cap + lax.rem(lax.broadcasted_iota(jnp.int32, (S, 128), 0), half_cap)
    chosen = hit & (rank == want.astype(F32))
    offset = jnp.sum(jnp.where(chosen, fields[1].astype(F32), 0.0), axis=1, keepdims=True)
    offset = offset.astype(jnp.int32)
    code = jnp.sum(jnp.where(chosen, fields[2].astype(F32), 0.0), axis=1, keepdims=True)
    lane = lax.broadcasted_iota(jnp.int32, (S, 128), 1)
    slots_ref[...] = jnp.where(lane == 0, offset, code.astype(jnp.int32))


def slot_table(desc, half_cap):
    S = desc.shape[0] * half_cap
    vm = pl.BlockSpec(memory_space=pltpu.VMEM)
    return pl.pallas_call(
        functools.partial(slot_kernel, half_cap),
        out_shape=jax.ShapeDtypeStruct((S, 128), jnp.int32),
        in_specs=[vm],
        out_specs=vm,
        scratch_shapes=[pltpu.VMEM((3, S, 128), jnp.int32)],
        compiler_params=pltpu.CompilerParams(vmem_limit_bytes=1024 * 1024),
        cost_estimate=pl.CostEstimate(flops=1_000_000, bytes_accessed=40_000, transcendentals=0),
        name="slot_table",
    )(desc)


def trunk_kernel(
    slots,
    genome,
    slots_ref,
    acts_ref,
    halo_ref,
    pair_ref,
    delta_ref,
    gain1_ref,
    gain2_ref,
    bias_ref,
    pair_bias_ref,
    conv1_ref,
    proj1_ref,
    conv2_ref,
    proj2_ref,
    head_ref,
    pair_head_ref,
    out_ref,
    xg,
    xalt,
    n1,
    g,
    h1,
    n2,
    h2,
):
    S = slots
    width, C = acts_ref.shape
    half = proj1_ref.shape[0]
    tracks = head_ref.shape[1]
    here = lax.axis_index("seq")
    core = lax.rem(lax.axis_index("rep"), 2)
    other = 1 - core

    offset = slots_ref[:, 0:1]
    code = slots_ref[:, 1:2]
    where_bin = here * width + offset

    def inside(j, m):
        at = where_bin + (j * D1 + m * D2)
        return (at >= 0) & (at < genome)

    sources = (
        (halo_ref, core * (REACH + width)),
        (acts_ref, REACH),
        (pair_ref, other * (REACH + width)),
    )
    picks = []
    for source, base in sources:
        column = lax.broadcasted_iota(jnp.int32, (S, source.shape[0]), 1) + base - offset
        picks.append(
            jnp.concatenate(
                [
                    jnp.where(column == a * D1 + m * D2, 1.0, 0.0).astype(BF16)
                    for a in range(5)
                    for m in range(5)
                ],
                axis=0,
            )
        )
    for n in range(C // NT):
        at = pl.ds(n * NT, NT)
        parts = [
            jnp.dot(picked, source[:, at], preferred_element_type=F32)
            for picked, (source, _) in zip(picks, sources)
        ]
        xg[:, at] = ((parts[0] + parts[1]) + parts[2]).astype(BF16)
    bump = jnp.zeros((S, C), F32)
    for k in range(4):
        bump = jnp.where(code == k, delta_ref[k : k + 1, :].astype(F32), bump)
    xalt[...] = xg[12 * S : 13 * S, :].astype(F32) + bump

    def normed(values, gain):
        scale = lax.rsqrt(jnp.mean(values * values, axis=-1, keepdims=True) + EPS)
        return (values * scale * gain).astype(BF16)

    gain1 = gain1_ref[...].astype(F32).reshape(1, C)
    for b in range(25):
        n1[b * S : (b + 1) * S, :] = normed(xg[b * S : (b + 1) * S, :].astype(F32), gain1)
    n1[25 * S : 26 * S, :] = normed(xalt[...], gain1)

    for n in range(half // NT):
        at = pl.ds(n * NT, NT)
        taps = []
        for k in range(3):
            left = jnp.concatenate(
                [n1[k * 5 * S : (k + 3) * 5 * S, :], n1[25 * S : 26 * S, :]], axis=0
            )
            taps.append(jnp.dot(left, conv1_ref[k, :, at], preferred_element_type=F32))
        total = (taps[0] + taps[1]) + taps[2]
        g[: 15 * S, at] = gelu(total[: 15 * S]).astype(BF16)
        for j in range(3):
            base = (j * 5 + 2) * S
            parts = [
                taps[k][15 * S : 16 * S] if k == 2 - j else taps[k][base : base + S]
                for k in range(3)
            ]
            g[(15 + j) * S : (16 + j) * S, at] = gelu((parts[0] + parts[1]) + parts[2]).astype(BF16)

    for n in range(C // NT):
        at = pl.ds(n * NT, NT)
        delta = jnp.dot(g[...], proj1_ref[:, at], preferred_element_type=F32)
        for j in range(3):
            for m in range(5):
                b = j * 5 + m
                x = xg[(b + 5) * S : (b + 6) * S, at].astype(F32)
                h = jnp.where(inside(j - 1, m - 2), x + delta[b * S : (b + 1) * S], 0.0)
                h1[(m * 3 + j) * S : (m * 3 + j + 1) * S, at] = h.astype(BF16)
            b = 15 + j
            x = xalt[:, at] if j == 1 else xg[(j * 5 + 7) * S : (j * 5 + 8) * S, at].astype(F32)
            h = jnp.where(inside(j - 1, 0), x + delta[b * S : (b + 1) * S], 0.0)
            h1[b * S : (b + 1) * S, at] = h.astype(BF16)
    gain2 = gain2_ref[...].astype(F32).reshape(1, C)
    for b in range(18):
        n2[b * S : (b + 1) * S, :] = normed(h1[b * S : (b + 1) * S, :].astype(F32), gain2)

    for n in range(half // NT):
        at = pl.ds(n * NT, NT)
        taps = []
        for k in range(3):
            left = jnp.concatenate(
                [n2[k * 3 * S : (k + 3) * 3 * S, :], n2[15 * S : 18 * S, :]], axis=0
            )
            taps.append(jnp.dot(left, conv2_ref[k, :, at], preferred_element_type=F32))
        total = (taps[0] + taps[1]) + taps[2]
        g[: 9 * S, at] = gelu(total[: 9 * S]).astype(BF16)
        for i in range(3):
            base = i * 3 * S
            parts = [
                taps[k][9 * S : 12 * S] if k == 2 - i else taps[k][base : base + 3 * S]
                for k in range(3)
            ]
            g[(9 + 3 * i) * S : (12 + 3 * i) * S, at] = gelu(
                (parts[0] + parts[1]) + parts[2]
            ).astype(BF16)

    for n in range(C // NT):
        at = pl.ds(n * NT, NT)
        delta = jnp.dot(g[...], proj2_ref[:, at], preferred_element_type=F32)
        for i in range(3):
            plain = h1[(i + 1) * 3 * S : (i + 2) * 3 * S, at].astype(F32)
            changed = h1[15 * S : 18 * S, at].astype(F32) if i == 1 else plain
            lo = i * 3 * S
            h2[lo : lo + 3 * S, at] = (plain + delta[lo : lo + 3 * S]).astype(BF16)
            lo += 9 * S
            h2[lo : lo + 3 * S, at] = (changed + delta[lo : lo + 3 * S]).astype(BF16)

    keep = [
        jnp.where(inside(j - 1, i - 1), 1.0, 0.0) for i in range(3) for j in range(3)
    ]
    for side in range(2):
        bias = (bias_ref, pair_bias_ref)[side][...].astype(F32).reshape(1, tracks)
        weight = (head_ref, pair_head_ref)[side]
        block = (core if side == 0 else other) * (S * (tracks // 128))
        for n in range(tracks // NT):
            at = pl.ds(n * NT, NT)
            logits = jnp.dot(h2[...], weight[:, at], preferred_element_type=F32)
            cover = softplus(logits + bias[:, n * NT : (n + 1) * NT])
            score = jnp.zeros((S, NT), F32)
            for b in range(9):
                change = cover[(9 + b) * S : (10 + b) * S] - cover[b * S : (b + 1) * S]
                score = score + change * keep[b]
            per = tracks // 128
            for t in range(NT // 128):
                start = block + n * (NT // 128) + t
                out_ref[pl.ds(start, S, stride=per), :] = score[:, t * 128 : (t + 1) * 128]


def trunk_and_head(table, acts, halo, pair, delta, gain1, gain2, bias, pair_bias, weights, genome):
    conv1, proj1, conv2, proj2, head, pair_head = weights
    S = table.shape[0]
    width, C = acts.shape
    half = proj1.shape[0]
    tracks = head.shape[1]
    vm = pl.BlockSpec(memory_space=pltpu.VMEM)
    macs = S * (48 * C * half + 18 * C * half + 36 * C * half + 18 * C * half + 36 * C * tracks)
    operands = [
        pltpu.with_memory_space_constraint(a, pltpu.VMEM)
        for a in (table, acts, halo, pair, delta, gain1, gain2, bias, pair_bias) + weights
    ]
    return pl.pallas_call(
        functools.partial(trunk_kernel, S, genome),
        out_shape=jax.ShapeDtypeStruct((2 * S * tracks // 128, 128), F32),
        in_specs=[vm] * len(operands),
        out_specs=vm,
        scratch_shapes=[
            pltpu.VMEM((25 * S, C), BF16),
            pltpu.VMEM((S, C), F32),
            pltpu.VMEM((26 * S, C), BF16),
            pltpu.VMEM((18 * S, half), BF16),
            pltpu.VMEM((18 * S, C), BF16),
            pltpu.VMEM((18 * S, C), BF16),
            pltpu.VMEM((18 * S, C), BF16),
        ],
        compiler_params=pltpu.CompilerParams(vmem_limit_bytes=12 * 1024 * 1024),
        cost_estimate=pl.CostEstimate(
            flops=2 * macs, bytes_accessed=28 * 1024 * 1024, transcendentals=S * 18 * (half * 2 + tracks * 4)
        ),
        name="trunk_and_head",
    )(*operands)


def return_kernel(n_seq, half_cap, owners_ref, got_ref, out_ref, tiles):
    count, tracks = out_ref.shape
    per = tracks // 128
    for v in range(count):
        mine = owners_ref[v]
        rank = jnp.int32(0)
        for u in range(v):
            rank = rank + jnp.where(owners_ref[u] == mine, 1, 0)
        side = lax.div(rank, half_cap)
        row = ((side * n_seq + mine) * half_cap + (rank - side * half_cap)) * per
        tiles[v * per : (v + 1) * per, :] = got_ref[pl.ds(pl.multiple_of(row, 8), per), :]
    for t in range(per):
        out_ref[:, t * 128 : (t + 1) * 128] = tiles[pl.ds(t, count, stride=per), :]


def first_kernel(acts_ref, owners_ref, offsets_ref, codes_ref, edge_ref, out_ref, rows, sem):
    core = lax.rem(lax.axis_index("rep"), 2)
    lists = out_ref.shape[0]
    count = owners_ref.shape[1]
    reach = edge_ref.shape[0]
    begin = pl.multiple_of((1 - core) * (acts_ref.shape[0] - reach), 16)
    copies = [pltpu.make_async_copy(acts_ref.at[pl.ds(begin, reach)], edge_ref, sem.at[3])]
    copies += [
        pltpu.make_async_copy(ref, row, sem.at[i])
        for i, (ref, row) in enumerate(zip((owners_ref, offsets_ref, codes_ref), rows))
    ]
    for copy in copies:
        copy.start()
    out_ref[...] = jnp.full(out_ref.shape, -1, jnp.int32)
    for copy in copies:
        copy.wait()
    for f in range(3):
        row = rows[f][...].reshape(1, count)
        for s in range(lists):
            out_ref[s, f : f + 1, 0:count] = row


def edge_and_lists(acts, owner, offsets, codes, lists):
    hbm = pl.BlockSpec(memory_space=pltpu.HBM)
    vm = pl.BlockSpec(memory_space=pltpu.VMEM)
    args = [pltpu.with_memory_space_constraint(a, pltpu.HBM) for a in (acts, owner, offsets, codes)]
    return pl.pallas_call(
        first_kernel,
        out_shape=(
            jax.ShapeDtypeStruct((REACH, acts.shape[1]), BF16),
            jax.ShapeDtypeStruct((lists, 8, 128), jnp.int32),
        ),
        in_specs=[hbm, hbm, hbm, hbm],
        out_specs=(vm, vm),
        scratch_shapes=[
            [pltpu.VMEM(a.shape, jnp.int32) for a in args[1:]],
            pltpu.SemaphoreType.DMA((4,)),
        ],
        compiler_params=pltpu.CompilerParams(vmem_limit_bytes=2 * 1024 * 1024),
        cost_estimate=pl.CostEstimate(flops=20_000_000_000, bytes_accessed=900_000, transcendentals=0),
        name="edge_and_lists",
    )(*args)


def per_device(
    reference_acts,
    owners,
    offsets,
    codes,
    base_delta,
    gain_one,
    conv_one,
    proj_one,
    gain_two,
    conv_two,
    proj_two,
    head_weight,
    head_bias,
):
    n_seq = lax.axis_size("seq")
    n_rep = lax.axis_size("rep")
    width = reference_acts.shape[0]
    genome = width * n_seq
    vcount = owners.shape[0]
    half_cap = max(2, 2 * vcount // n_seq) // 2
    tracks = head_weight.shape[1]
    swap = [(r, r ^ 1) for r in range(n_rep)]
    steps = [(i, r, i + 1 - 2 * (r % 2)) for i in range(n_seq) for r in range(n_rep)]
    edges = [(i * n_rep + r, j * n_rep + r) for i, r, j in steps if 0 <= j < n_seq]

    owner = owners[:, 0]
    edge, fields = edge_and_lists(
        reference_acts, owners.reshape(1, vcount), offsets, codes, n_seq
    )
    halo = lax.ppermute(edge, ("seq", "rep"), edges)
    pair_head = lax.ppermute(head_weight, "rep", swap)
    pair_bias = lax.ppermute(head_bias, "rep", swap)
    desc = lax.all_to_all(fields, "seq", split_axis=0, concat_axis=0, tiled=True)
    halo, desc = lax.optimization_barrier((halo, desc))
    pair = lax.ppermute(halo, "rep", swap)
    scores = trunk_and_head(
        slot_table(desc, half_cap),
        reference_acts,
        halo,
        pair,
        base_delta,
        gain_one,
        gain_two,
        head_bias,
        pair_bias,
        (conv_one, proj_one, conv_two, proj_two, head_weight, pair_head),
        genome,
    )
    per = tracks // 128
    groups = [
        [s * n_rep + x + c for c in range(2) for s in range(n_seq)] for x in range(0, n_rep, 2)
    ]
    got = lax.all_to_all(
        scores.reshape(2 * n_seq, half_cap * per, 128),
        ("seq", "rep"),
        split_axis=0,
        concat_axis=0,
        axis_index_groups=groups,
        tiled=True,
    ).reshape(2 * n_seq * half_cap * per, 128)
    got = pltpu.with_memory_space_constraint(got, pltpu.VMEM)
    return pl.pallas_call(
        functools.partial(return_kernel, n_seq, half_cap),
        out_shape=jax.ShapeDtypeStruct((vcount, tracks), F32),
        in_specs=[pl.BlockSpec(memory_space=pltpu.SMEM), pl.BlockSpec(memory_space=pltpu.VMEM)],
        out_specs=pl.BlockSpec(memory_space=pltpu.VMEM),
        scratch_shapes=[pltpu.VMEM((vcount * per, 128), F32)],
        compiler_params=pltpu.CompilerParams(vmem_limit_bytes=2 * 1024 * 1024),
        name="pick_scores",
    )(owner, got)


def solution(mesh):
    return jax.shard_map(
        per_device,
        mesh=mesh,
        in_specs=(
            P("seq", None),
            P("seq", None),
            P("seq"),
            P("seq"),
            P(),
            P(),
            P(),
            P(),
            P(),
            P(),
            P(),
            P(None, "rep"),
            P("rep"),
        ),
        out_specs=P("seq", "rep"),
        check_vma=False,
    )
```

time: 48 us -> 45.1 us (0.940)
  Pallas kernels: 15.6 us -> 13.5 us
  local copies, waits for them, and re-layouts: 1.06 us -> 0.05 us
  other arithmetic: 0.7 us -> 0.01 us
  blocking collectives: 23.6 us -> 24.2 us
    pallas_call x1 -> x3, Pallas kernels: 13.9 us -> 12.1 us  [the longest x1 10.7 us: trunk_and_head(): pl.pallas_call(functools.partial(trunk_kernel, S, genome), out_shape=jax....]
    dynamic_slice x1 -> x0, local copies, waits for them, and re-layouts: 1.04 us -> none  [per_device(): lax.dynamic_slice_in_dim(reference_acts, (1 - core) * (width - REACH), RE...]
    another operation x1 -> x0, other arithmetic: 0.7 us -> none  [per_device(): fields = jnp.stack([owner, offsets, codes])]
  transfers between devices with their start and end apart: 4 -> 4, of which waited for: 2 -> 1; matrix products, arithmetic and copies ran while one was open for 4% -> 0% of each run, Pallas kernels for 0% -> 3%
where the time goes in v1:
time: 45.1 us; the launch traced here: 44.8 us
  blocking collectives  24.2 us (54%)
  Pallas kernels  13.5 us (30%)
  starting transfers between devices  5.82 us (13%)
  waiting for transfers between devices  1.07 us (2%)
    all_to_all x1, blocking collectives, per_device(): lax.all_to_all(scores.reshape(2 * n_seq, half_cap * per, 128), ('seq', 'r...  12.6 us
    all_to_all x1, blocking collectives, per_device(): lax.all_to_all(fields, 'seq', split_axis=0, concat_axis=0, tiled=True)  11.6 us
    pallas_call x1, Pallas kernels, trunk_and_head(): pl.pallas_call(functools.partial(trunk_kernel, S, genome), out_shape=jax....  10.7 us
    ppermute x1, starting transfers between devices, per_device(): halo = lax.ppermute(edge, ('seq', 'rep'), edges)  4.86 us
    pallas_call x1, Pallas kernels, per_device(): pl.pallas_call(functools.partial(return_kernel, n_seq, half_cap), out_sha...  1.37 us
    pallas_call x1, Pallas kernels, edge_and_lists(): pl.pallas_call(first_kernel, out_shape=(jax.ShapeDtypeStruct((REACH, acts...  1.22 us
    ppermute x1, waiting for transfers between devices, per_device(): pair_bias = lax.ppermute(head_bias, 'rep', swap)  1.06 us
  transfers between devices with their start and end apart: 4, of which 1 were waited for; matrix products, arithmetic and copies ran while one was open for 0% of the time, Pallas kernels for 3%

profile of v1, /device:TPU:0, one launch (start us, length us, event | category | flops | bytes accessed | tf_op | source)
XLA Modules:
  0.0 44.8 jit_solution(8043348528211435854)
XLA Ops:
  0.0 0.5 %collective-permute-start.3 = (bf16[1536,1024]{1,0:T(8,128)(2,1)}, bf16[1536,1024]{1,0:T(8,128)(2,1)S(1)}, u32[]{:S(2)}, u32[]{:S(2)}) collective-permute-start(bf16[1536,1024]{1,0:T(8,128)(2,1)} %head_ref.1), channel_id=1, source_target_pairs={{0,1},{1,0},{2,3},{3,2},{4,5},{5,4},{6,7},{7,6},{8,9},{9,8},{10,11... | collective-permute-start | bytes 9437192 | tf_op jit(solution)/shard_map/ppermute | solution.py:365
  0.5 0.0 slice-start.3
  0.5 0.0 copy-start
  0.5 0.0 copy-start.1
  0.5 0.0 copy-start.2
  0.5 0.0 copy-start.3
  0.5 0.0 copy-start.4
  0.5 0.0 copy-start.5
  0.5 0.0 copy-start.6
  0.5 1.2 %edge_and_lists.1 = (bf16[144,1536]{1,0:T(8,128)(2,1)S(1)}, s32[8,8,128]{2,1,0:T(8,128)S(1)}) custom-call(bf16[256,1536]{1,0:T(8,128)(2,1)} %acts_ref.3, s32[1,16]{1,0:T(1,128)} %bitcast.10, s32[16]{0:T(128)} %offsets_ref.1, s32[16]{0:T(128)} %codes_ref.1), custom_call_target="tpu_custom_call" | custom-call | flops 20000000000 | bytes 900000 | tf_op jit(solution)/shard_map/edge_and_lists/pallas_call | solution.py:316
  1.8 4.9 %collective-permute-start = (bf16[144,1536]{1,0:T(8,128)(2,1)S(1)}, bf16[144,1536]{1,0:T(8,128)(2,1)S(1)}, u32[]{:S(2)}, u32[]{:S(2)}) collective-permute-start(bf16[144,1536]{1,0:T(8,128)(2,1)S(1)} %get-tuple-element.9), channel_id=1, source_target_pairs={{0,4},{2,6},{4,8},{5,1},{6,10},{7,3},{8,12},{9,5},{10,14},{11,7},{... | collective-permute-start | bytes 1327112 | tf_op jit(solution)/shard_map/ppermute | solution.py:364
  6.6 11.6 %all_to_all.10.desc_ref = s32[8,8,128]{2,1,0:T(8,128)S(1)} all-to-all(s32[8,8,128]{2,1,0:T(8,128)S(1)} %get-tuple-element.10), channel_id=1, replica_groups=mesh['seq'=8,'rep'=4] {'seq'}, dimensions={0} | all-to-all | bytes 65536 | tf_op jit(solution)/shard_map/all_to_all | solution.py:367
  18.2 0.0 collective-permute-done.halo_ref
  18.3 0.0 collective-permute-start.1
  18.3 0.0 copy-done.7
  18.3 0.5 %collective-permute-start.2 = (bf16[1024]{0:T(1024)(128)(2,1)S(1)}, bf16[1024]{0:T(1024)(128)(2,1)S(1)}, u32[]{:S(2)}, u32[]{:S(2)}) collective-permute-start(bf16[1024]{0:T(1024)(128)(2,1)S(1)} %copy-done.7), channel_id=1, source_target_pairs={{0,1},{1,0},{2,3},{3,2},{4,5},{5,4},{6,7},{7,6},{8,9},{9,8},{10,11... | collective-permute-start | bytes 6152 | tf_op jit(solution)/shard_map/ppermute | solution.py:366
  18.8 0.2 slot_table.1.slots_ref
  19.0 1.1 %collective-permute-done.2.pair_bias_ref = bf16[1024]{0:T(1024)(128)(2,1)S(1)} collective-permute-done((bf16[1024]{0:T(1024)(128)(2,1)S(1)}, bf16[1024]{0:T(1024)(128)(2,1)S(1)}, u32[]{:S(2)}, u32[]{:S(2)}) %collective-permute-start.2) | collective-permute-done | bytes 2080 | tf_op jit(solution)/shard_map/ppermute | solution.py:366
  20.0 0.0 collective-permute-done.1.pair_ref
  20.0 0.0 collective-permute-done.3.pair_head_ref
  20.1 0.0 slice-done
  20.1 0.0 slice-done.2
  20.1 0.0 slice-done.1
  20.1 0.0 slice-done.3
  20.1 0.0 copy-done
  20.1 0.0 copy-done.1
  20.1 0.0 copy-done.2
  20.1 0.0 copy-done.3
  20.1 0.0 copy-done.4
  20.2 10.7 %trunk_and_head.1 = f32[256,128]{1,0:T(8,128)S(1)} custom-call(s32[16,128]{1,0:T(8,128)S(1)} %slot_table.1.slots_ref, bf16[256,1536]{1,0:T(8,128)(2,1)S(1)} %copy-done.3, bf16[144,1536]{1,0:T(8,128)(2,1)S(1)} %collective-permute-done.halo_ref, bf16[144,1536]{1,0:T(8,128)(2,1)S(1)} %collective-permute-done.1.pair_ref, bf16[4,1536]{1,0:T(4,128)(2,1)S(1)} %copy-done.4, ...), custom_call_target="tpu_custom_call" | custom-call | flops 6341787648 | bytes 29360128 | tf_op jit(solution)/shard_map/trunk_and_head/pallas_call | solution.py:253
  30.8 12.6 %all_to_all.11 = f32[16,16,128]{2,1,0:T(8,128)S(1)} all-to-all(f32[16,16,128]{2,1,0:T(8,128)S(1)} %bitcast.8), channel_id=1, replica_groups={{0,4,8,12,16,20,24,28,1,5,9,13,17,21,25,29},{2,6,10,14,18,22,26,30,3,7,..., dimensions={0} | all-to-all | bytes 262144 | tf_op jit(solution)/shard_map/all_to_all | solution.py:387
  43.5 1.4 %pick_scores.1 = f32[16,1024]{1,0:T(8,128)} custom-call(s32[16]{0:T(128)S(1)} %bitcast.11, f32[256,128]{1,0:T(8,128)S(1)} %bitcast.9), custom_call_target="tpu_custom_call" | custom-call | tf_op jit(solution)/shard_map/pick_scores/pallas_call | solution.py:396
  (10 shorter events, 0.0 us)
Async XLA Ops:
  0.0 20.1 %collective-permute-start.3 = (bf16[1536,1024]{1,0:T(8,128)(2,1)}, bf16[1536,1024]{1,0:T(8,128)(2,1)S(1)}, u32[]{:S(2)}, u32[]{:S(2)}) collective-permute-start(bf16[1536,1024]{1,0:T(8,128)(2,1)} %head_ref.1), channel_id=1, source_target_pairs={{0,1},{1,0},{2,3},{3,2},{4,5},{5,4},{6,7},{7,6},{8,9},{9,8},{10,11... | collective-permute-start | bytes 9437192 | tf_op jit(solution)/shard_map/ppermute | solution.py:365
  0.5 19.6 %slice-start = ((s8[7077888]{0:T(1024)(128)(4,1)}), s8[4194304]{0:T(1024)(128)(4,1)S(1)}, s32[]{:S(2)}) async-start(s8[7077888]{0:T(1024)(128)(4,1)} %bitcast.4), calls=%async_computation.2 | async-start | bytes 8388608
  0.5 19.6 %slice-start.2 = ((s8[7077888]{0:T(1024)(128)(4,1)}), s8[4194304]{0:T(1024)(128)(4,1)S(1)}, s32[]{:S(2)}) async-start(s8[7077888]{0:T(1024)(128)(4,1)} %bitcast.6), calls=%async_computation.4 | async-start | bytes 8388608
  0.5 17.8 %copy-start.7 = (bf16[1024]{0:T(1024)(128)(2,1)S(1)}, bf16[1024]{0:T(1024)(128)(2,1)}, u32[]{:S(2)}) copy-start(bf16[1024]{0:T(1024)(128)(2,1)} %bias_ref.1) | copy-start | bytes 6148
  0.5 19.6 %slice-start.1 = ((s8[7077888]{0:T(1024)(128)(4,1)}), s8[2883584]{0:T(1024)(128)(4,1)S(1)}, s32[]{:S(2)}) async-start(s8[7077888]{0:T(1024)(128)(4,1)} %bitcast.4), calls=%async_computation.3 | async-start | bytes 5767168
  0.5 19.6 %slice-start.3 = ((s8[7077888]{0:T(1024)(128)(4,1)}), s8[2883584]{0:T(1024)(128)(4,1)S(1)}, s32[]{:S(2)}) async-start(s8[7077888]{0:T(1024)(128)(4,1)} %bitcast.6), calls=%async_computation.5 | async-start | bytes 5767168
  0.5 19.6 %copy-start = (bf16[1536,1024]{1,0:T(8,128)(2,1)S(1)}, bf16[1536,1024]{1,0:T(8,128)(2,1)}, u32[]{:S(2)}) copy-start(bf16[1536,1024]{1,0:T(8,128)(2,1)} %head_ref.1) | copy-start | bytes 9437188
  0.5 19.6 %copy-start.1 = (bf16[768,1536]{1,0:T(8,128)(2,1)S(1)}, bf16[768,1536]{1,0:T(8,128)(2,1)}, u32[]{:S(2)}) copy-start(bf16[768,1536]{1,0:T(8,128)(2,1)} %proj1_ref.1) | copy-start | bytes 7077892
  0.5 19.6 %copy-start.2 = (bf16[768,1536]{1,0:T(8,128)(2,1)S(1)}, bf16[768,1536]{1,0:T(8,128)(2,1)}, u32[]{:S(2)}) copy-start(bf16[768,1536]{1,0:T(8,128)(2,1)} %proj2_ref.1) | copy-start | bytes 7077892
  0.5 19.6 %copy-start.3 = (bf16[256,1536]{1,0:T(8,128)(2,1)S(1)}, bf16[256,1536]{1,0:T(8,128)(2,1)}, u32[]{:S(2)}) copy-start(bf16[256,1536]{1,0:T(8,128)(2,1)} %acts_ref.3) | copy-start | bytes 2359300
  0.5 19.6 %copy-start.4 = (bf16[4,1536]{1,0:T(4,128)(2,1)S(1)}, bf16[4,1536]{1,0:T(4,128)(2,1)}, u32[]{:S(2)}) copy-start(bf16[4,1536]{1,0:T(4,128)(2,1)} %delta_ref.1) | copy-start | bytes 36868
  0.5 19.6 %copy-start.5 = (bf16[1536]{0:T(1024)(128)(2,1)S(1)}, bf16[1536]{0:T(1024)(128)(2,1)}, u32[]{:S(2)}) copy-start(bf16[1536]{0:T(1024)(128)(2,1)} %gain1_ref.1) | copy-start | bytes 9220
  0.5 19.6 %copy-start.6 = (bf16[1536]{0:T(1024)(128)(2,1)S(1)}, bf16[1536]{0:T(1024)(128)(2,1)}, u32[]{:S(2)}) copy-start(bf16[1536]{0:T(1024)(128)(2,1)} %gain2_ref.1) | copy-start | bytes 9220
  1.8 16.5 %collective-permute-start = (bf16[144,1536]{1,0:T(8,128)(2,1)S(1)}, bf16[144,1536]{1,0:T(8,128)(2,1)S(1)}, u32[]{:S(2)}, u32[]{:S(2)}) collective-permute-start(bf16[144,1536]{1,0:T(8,128)(2,1)S(1)} %get-tuple-element.9), channel_id=1, source_target_pairs={{0,4},{2,6},{4,8},{5,1},{6,10},{7,3},{8,12},{9,5},{10,14},{11,7},{... | collective-permute-start | bytes 1327112 | tf_op jit(solution)/shard_map/ppermute | solution.py:364
  18.3 1.8 %collective-permute-start.1 = (bf16[144,1536]{1,0:T(8,128)(2,1)S(1)}, bf16[144,1536]{1,0:T(8,128)(2,1)S(1)}, u32[]{:S(2)}, u32[]{:S(2)}) collective-permute-start(bf16[144,1536]{1,0:T(8,128)(2,1)S(1)} %collective-permute-done.halo_ref), channel_id=1, source_target_pairs={{0,1},{1,0},{2,3},{3,2},{4,5},{5,4},{6,7},{7,6},{8,9},{9,8},{10,11... | collective-permute-start | bytes 1327112 | tf_op jit(solution)/shard_map/ppermute | solution.py:369
  18.3 1.8 %collective-permute-start.2 = (bf16[1024]{0:T(1024)(128)(2,1)S(1)}, bf16[1024]{0:T(1024)(128)(2,1)S(1)}, u32[]{:S(2)}, u32[]{:S(2)}) collective-permute-start(bf16[1024]{0:T(1024)(128)(2,1)S(1)} %copy-done.7), channel_id=1, source_target_pairs={{0,1},{1,0},{2,3},{3,2},{4,5},{5,4},{6,7},{7,6},{8,9},{9,8},{10,11... | collective-permute-start | bytes 6152 | tf_op jit(solution)/shard_map/ppermute | solution.py:366
  19.0 24.5 %copy-start.8 = (s32[16,1]{0,1:T(1,128)S(1)}, s32[16,1]{0,1:T(1,128)}, u32[]{:S(2)}) copy-start(s32[16,1]{0,1:T(1,128)} %param.14) | copy-start | bytes 196

commit v2 on v1

--- a/solution.py
+++ b/solution.py
@@ -22,10 +22,25 @@
 
 
 def softplus(x):
-    return jnp.maximum(x, 0.0) + jnp.log1p(jnp.exp(-jnp.abs(x)))
-
-
-def slot_kernel(half_cap, desc_ref, slots_ref, fields):
+    return jnp.maximum(x, 0.0) + jnp.log(1.0 + jnp.exp(-jnp.abs(x)))
+
+
+def pick_rows(offset, count, base):
+    S = offset.shape[0]
+    column = lax.broadcasted_iota(jnp.int32, (S, count), 1) + base - offset
+    return jnp.concatenate(
+        [
+            jnp.where(column == a * D1 + m * D2, 1.0, 0.0).astype(BF16)
+            for a in range(5)
+            for m in range(5)
+        ],
+        axis=0,
+    )
+
+
+def slot_kernel(
+    half_cap, per, desc_ref, acts_ref, halo_ref, slots_ref, places_ref, early_ref, fields
+):
     lists = desc_ref.shape[0]
     S = lists * half_cap
     here = lax.axis_index("seq")
@@ -53,28 +68,56 @@
     lane = lax.broadcasted_iota(jnp.int32, (S, 128), 1)
     slots_ref[...] = jnp.where(lane == 0, offset, code.astype(jnp.int32))
 
-
-def slot_table(desc, half_cap):
+    width, C = acts_ref.shape
+    own = pick_rows(offset, width, REACH)
+    near = pick_rows(offset, halo_ref.shape[0], core * (REACH + width))
+    for n in range(C // NT):
+        at = pl.ds(n * NT, NT)
+        found = jnp.dot(own, acts_ref[:, at], preferred_element_type=F32)
+        found = found + jnp.dot(near, halo_ref[:, at], preferred_element_type=F32)
+        early_ref[:, at] = found.astype(BF16)
+
+    window = lax.broadcasted_iota(jnp.int32, (lists, 128), 0)
+    hit = jnp.broadcast_to(desc_ref[here, 0:1, :], (lists, 128)) == window
+    rank = jnp.dot(
+        jnp.where(hit, 1.0, 0.0).astype(BF16),
+        jnp.where(upper, 1.0, 0.0).astype(BF16),
+        preferred_element_type=F32,
+    ).astype(jnp.int32)
+    side = jnp.where(rank >= half_cap, 1, 0)
+    place = ((side * lists + window) * half_cap + (rank - side * half_cap)) * per
+    place = jnp.sum(jnp.where(hit, place.astype(F32), 0.0), axis=0, keepdims=True)
+    places_ref[...] = jnp.broadcast_to(place.astype(jnp.int32), places_ref.shape)
+
+
+def slot_table(desc, acts, halo, half_cap, per):
     S = desc.shape[0] * half_cap
+    acts, halo = (pltpu.with_memory_space_constraint(a, pltpu.VMEM) for a in (acts, halo))
     vm = pl.BlockSpec(memory_space=pltpu.VMEM)
     return pl.pallas_call(
-        functools.partial(slot_kernel, half_cap),
-        out_shape=jax.ShapeDtypeStruct((S, 128), jnp.int32),
-        in_specs=[vm],
-        out_specs=vm,
+        functools.partial(slot_kernel, half_cap, per),
+        out_shape=(
+            jax.ShapeDtypeStruct((S, 128), jnp.int32),
+            jax.ShapeDtypeStruct((8, 128), jnp.int32),
+            jax.ShapeDtypeStruct((25 * S, acts.shape[1]), BF16),
+        ),
+        in_specs=[vm, vm, vm],
+        out_specs=(vm, vm, vm),
         scratch_shapes=[pltpu.VMEM((3, S, 128), jnp.int32)],
-        compiler_params=pltpu.CompilerParams(vmem_limit_bytes=1024 * 1024),
-        cost_estimate=pl.CostEstimate(flops=1_000_000, bytes_accessed=40_000, transcendentals=0),
+        compiler_params=pltpu.CompilerParams(vmem_limit_bytes=4 * 1024 * 1024),
+        cost_estimate=pl.CostEstimate(
+            flops=50 * S * acts.shape[1] * (acts.shape[0] + REACH), bytes_accessed=2_000_000, transcendentals=0
+        ),
         name="slot_table",
-    )(desc)
+    )(desc, acts, halo)
 
 
 def trunk_kernel(
     slots,
+    width,
     genome,
     slots_ref,
-    acts_ref,
-    halo_ref,
+    early_ref,
     pair_ref,
     delta_ref,
     gain1_ref,
@@ -97,7 +140,7 @@
     h2,
 ):
     S = slots
-    width, C = acts_ref.shape
+    C = early_ref.shape[1]
     half = proj1_ref.shape[0]
     tracks = head_ref.shape[1]
     here = lax.axis_index("seq")
@@ -112,31 +155,11 @@
         at = where_bin + (j * D1 + m * D2)
         return (at >= 0) & (at < genome)
 
-    sources = (
-        (halo_ref, core * (REACH + width)),
-        (acts_ref, REACH),
-        (pair_ref, other * (REACH + width)),
-    )
-    picks = []
-    for source, base in sources:
-        column = lax.broadcasted_iota(jnp.int32, (S, source.shape[0]), 1) + base - offset
-        picks.append(
-            jnp.concatenate(
-                [
-                    jnp.where(column == a * D1 + m * D2, 1.0, 0.0).astype(BF16)
-                    for a in range(5)
-                    for m in range(5)
-                ],
-                axis=0,
-            )
-        )
+    chosen = pick_rows(offset, pair_ref.shape[0], other * (REACH + width))
     for n in range(C // NT):
         at = pl.ds(n * NT, NT)
-        parts = [
-            jnp.dot(picked, source[:, at], preferred_element_type=F32)
-            for picked, (source, _) in zip(picks, sources)
-        ]
-        xg[:, at] = ((parts[0] + parts[1]) + parts[2]).astype(BF16)
+        found = jnp.dot(chosen, pair_ref[:, at], preferred_element_type=F32)
+        xg[:, at] = (found + early_ref[:, at].astype(F32)).astype(BF16)
     bump = jnp.zeros((S, C), F32)
     for k in range(4):
         bump = jnp.where(code == k, delta_ref[k : k + 1, :].astype(F32), bump)
@@ -238,20 +261,20 @@
                 out_ref[pl.ds(start, S, stride=per), :] = score[:, t * 128 : (t + 1) * 128]
 
 
-def trunk_and_head(table, acts, halo, pair, delta, gain1, gain2, bias, pair_bias, weights, genome):
+def trunk_and_head(table, early, pair, delta, gain1, gain2, bias, pair_bias, weights, width, genome):
     conv1, proj1, conv2, proj2, head, pair_head = weights
     S = table.shape[0]
-    width, C = acts.shape
+    C = early.shape[1]
     half = proj1.shape[0]
     tracks = head.shape[1]
     vm = pl.BlockSpec(memory_space=pltpu.VMEM)
     macs = S * (48 * C * half + 18 * C * half + 36 * C * half + 18 * C * half + 36 * C * tracks)
     operands = [
         pltpu.with_memory_space_constraint(a, pltpu.VMEM)
-        for a in (table, acts, halo, pair, delta, gain1, gain2, bias, pair_bias) + weights
+        for a in (table, early, pair, delta, gain1, gain2, bias, pair_bias) + weights
     ]
     return pl.pallas_call(
-        functools.partial(trunk_kernel, S, genome),
+        functools.partial(trunk_kernel, S, width, genome),
         out_shape=jax.ShapeDtypeStruct((2 * S * tracks // 128, 128), F32),
         in_specs=[vm] * len(operands),
         out_specs=vm,
@@ -272,29 +295,20 @@
     )(*operands)
 
 
-def return_kernel(n_seq, half_cap, owners_ref, got_ref, out_ref, tiles):
+def return_kernel(places_ref, got_ref, out_ref, tiles):
     count, tracks = out_ref.shape
     per = tracks // 128
     for v in range(count):
-        mine = owners_ref[v]
-        rank = jnp.int32(0)
-        for u in range(v):
-            rank = rank + jnp.where(owners_ref[u] == mine, 1, 0)
-        side = lax.div(rank, half_cap)
-        row = ((side * n_seq + mine) * half_cap + (rank - side * half_cap)) * per
-        tiles[v * per : (v + 1) * per, :] = got_ref[pl.ds(pl.multiple_of(row, 8), per), :]
+        row = pl.multiple_of(places_ref[v], 8)
+        tiles[v * per : (v + 1) * per, :] = got_ref[pl.ds(row, per), :]
     for t in range(per):
         out_ref[:, t * 128 : (t + 1) * 128] = tiles[pl.ds(t, count, stride=per), :]
 
 
-def first_kernel(acts_ref, owners_ref, offsets_ref, codes_ref, edge_ref, out_ref, rows, sem):
-    core = lax.rem(lax.axis_index("rep"), 2)
+def pack_kernel(owners_ref, offsets_ref, codes_ref, out_ref, rows, sem):
     lists = out_ref.shape[0]
     count = owners_ref.shape[1]
-    reach = edge_ref.shape[0]
-    begin = pl.multiple_of((1 - core) * (acts_ref.shape[0] - reach), 16)
-    copies = [pltpu.make_async_copy(acts_ref.at[pl.ds(begin, reach)], edge_ref, sem.at[3])]
-    copies += [
+    copies = [
         pltpu.make_async_copy(ref, row, sem.at[i])
         for i, (ref, row) in enumerate(zip((owners_ref, offsets_ref, codes_ref), rows))
     ]
@@ -309,25 +323,21 @@
             out_ref[s, f : f + 1, 0:count] = row
 
 
-def edge_and_lists(acts, owner, offsets, codes, lists):
+def pack_lists(owner, offsets, codes, lists):
     hbm = pl.BlockSpec(memory_space=pltpu.HBM)
-    vm = pl.BlockSpec(memory_space=pltpu.VMEM)
-    args = [pltpu.with_memory_space_constraint(a, pltpu.HBM) for a in (acts, owner, offsets, codes)]
+    args = [pltpu.with_memory_space_constraint(a, pltpu.HBM) for a in (owner, offsets, codes)]
     return pl.pallas_call(
-        first_kernel,
-        out_shape=(
-            jax.ShapeDtypeStruct((REACH, acts.shape[1]), BF16),
-            jax.ShapeDtypeStruct((lists, 8, 128), jnp.int32),
-        ),
-        in_specs=[hbm, hbm, hbm, hbm],
-        out_specs=(vm, vm),
+        pack_kernel,
+        out_shape=jax.ShapeDtypeStruct((lists, 8, 128), jnp.int32),
+        in_specs=[hbm, hbm, hbm],
+        out_specs=pl.BlockSpec(memory_space=pltpu.VMEM),
         scratch_shapes=[
-            [pltpu.VMEM(a.shape, jnp.int32) for a in args[1:]],
-            pltpu.SemaphoreType.DMA((4,)),
+            [pltpu.VMEM(a.shape, jnp.int32) for a in args],
+            pltpu.SemaphoreType.DMA((3,)),
         ],
-        compiler_params=pltpu.CompilerParams(vmem_limit_bytes=2 * 1024 * 1024),
-        cost_estimate=pl.CostEstimate(flops=20_000_000_000, bytes_accessed=900_000, transcendentals=0),
-        name="edge_and_lists",
+        compiler_params=pltpu.CompilerParams(vmem_limit_bytes=1024 * 1024),
+        cost_estimate=pl.CostEstimate(flops=20_000_000_000, bytes_accessed=40_000, transcendentals=0),
+        name="pack_lists",
     )(*args)
 
 
@@ -357,20 +367,20 @@
     steps = [(i, r, i + 1 - 2 * (r % 2)) for i in range(n_seq) for r in range(n_rep)]
     edges = [(i * n_rep + r, j * n_rep + r) for i, r, j in steps if 0 <= j < n_seq]
 
-    owner = owners[:, 0]
-    edge, fields = edge_and_lists(
-        reference_acts, owners.reshape(1, vcount), offsets, codes, n_seq
-    )
+    fields = pack_lists(owners.reshape(1, vcount), offsets, codes, n_seq)
+    core = lax.axis_index("rep") % 2
+    edge = lax.dynamic_slice_in_dim(reference_acts, (1 - core) * (width - REACH), REACH, 0)
     halo = lax.ppermute(edge, ("seq", "rep"), edges)
     pair_head = lax.ppermute(head_weight, "rep", swap)
     pair_bias = lax.ppermute(head_bias, "rep", swap)
     desc = lax.all_to_all(fields, "seq", split_axis=0, concat_axis=0, tiled=True)
     halo, desc = lax.optimization_barrier((halo, desc))
     pair = lax.ppermute(halo, "rep", swap)
+    per = tracks // 128
+    slots, places, early = slot_table(desc, reference_acts, halo, half_cap, per)
     scores = trunk_and_head(
-        slot_table(desc, half_cap),
-        reference_acts,
-        halo,
+        slots,
+        early,
         pair,
         base_delta,
         gain_one,
@@ -378,9 +388,9 @@
         head_bias,
         pair_bias,
         (conv_one, proj_one, conv_two, proj_two, head_weight, pair_head),
+        width,
         genome,
     )
-    per = tracks // 128
     groups = [
         [s * n_rep + x + c for c in range(2) for s in range(n_seq)] for x in range(0, n_rep, 2)
     ]
@@ -394,14 +404,14 @@
     ).reshape(2 * n_seq * half_cap * per, 128)
     got = pltpu.with_memory_space_constraint(got, pltpu.VMEM)
     return pl.pallas_call(
-        functools.partial(return_kernel, n_seq, half_cap),
+        return_kernel,
         out_shape=jax.ShapeDtypeStruct((vcount, tracks), F32),
         in_specs=[pl.BlockSpec(memory_space=pltpu.SMEM), pl.BlockSpec(memory_space=pltpu.VMEM)],
         out_specs=pl.BlockSpec(memory_space=pltpu.VMEM),
         scratch_shapes=[pltpu.VMEM((vcount * per, 128), F32)],
         compiler_params=pltpu.CompilerParams(vmem_limit_bytes=2 * 1024 * 1024),
         name="pick_scores",
-    )(owner, got)
+    )(places[0], got)
 
 
 def solution(mesh):

time: 45.1 us -> 43.8 us (0.971)
  blocking collectives: 24.2 us -> 11.6 us
  waiting for transfers between devices: 1.07 us -> 7.92 us
  starting transfers between devices: 5.82 us -> 9.57 us
  local copies, waits for them, and re-layouts: 0.05 us -> 1.12 us
    all_to_all x1 -> x0, blocking collectives: 12.6 us -> none  [per_device(): lax.all_to_all(scores.reshape(2 * n_seq, half_cap * per, 128), ('seq', 'r...]
    all_to_all x0 -> x1, waiting for transfers between devices: none -> 7.66 us  [per_device(): lax.all_to_all(scores.reshape(2 * n_seq, half_cap * per, 128), ('seq', 'r...]
    all_to_all x0 -> x1, starting transfers between devices: none -> 4.16 us  [per_device(): lax.all_to_all(scores.reshape(2 * n_seq, half_cap * per, 128), ('seq', 'r...]
    dynamic_slice x0 -> x1, local copies, waits for them, and re-layouts: none -> 1.04 us  [per_device(): lax.dynamic_slice_in_dim(reference_acts, (1 - core) * (width - REACH), RE...]
    ppermute x1, waiting for transfers between devices: 1.06 us -> 0.25 us  [per_device(): pair_bias = lax.ppermute(head_bias, 'rep', swap)]
  transfers between devices with their start and end apart: 4 -> 5, of which waited for: 1 -> 2; matrix products, arithmetic and copies ran while one was open for 0% -> 2% of each run, Pallas kernels for 3% -> 4%
where the time goes in v2:
time: 43.8 us; the launch traced here: 43.5 us
  Pallas kernels  13.1 us (30%)
  blocking collectives  11.6 us (26%)
  starting transfers between devices  9.57 us (22%)
  waiting for transfers between devices  7.92 us (18%)
  local copies, waits for them, and re-layouts  1.12 us (3%)
    all_to_all x1, blocking collectives, per_device(): lax.all_to_all(fields, 'seq', split_axis=0, concat_axis=0, tiled=True)  11.6 us
    pallas_call x1, Pallas kernels, trunk_and_head(): pl.pallas_call(functools.partial(trunk_kernel, S, width, genome), out_sha...  9.99 us
    all_to_all x1, waiting for transfers between devices, per_device(): lax.all_to_all(scores.reshape(2 * n_seq, half_cap * per, 128), ('seq', 'r...  7.66 us
    ppermute x1, starting transfers between devices, per_device(): halo = lax.ppermute(edge, ('seq', 'rep'), edges)  4.45 us
    all_to_all x1, starting transfers between devices, per_device(): lax.all_to_all(scores.reshape(2 * n_seq, half_cap * per, 128), ('seq', 'r...  4.16 us
    pallas_call x1, Pallas kernels, per_device(): pl.pallas_call(return_kernel, out_shape=jax.ShapeDtypeStruct((vcount, tra...  1.2 us
    dynamic_slice x1, local copies, waits for them, and re-layouts, per_device(): lax.dynamic_slice_in_dim(reference_acts, (1 - core) * (width - REACH), RE...  1.04 us
    pallas_call x1, Pallas kernels, slot_table(): pl.pallas_call(functools.partial(slot_kernel, half_cap, per), out_shape=(...  1.02 us
  transfers between devices with their start and end apart: 5, of which 2 were waited for; matrix products, arithmetic and copies ran while one was open for 2% of the time, Pallas kernels for 4%

profile of v2, /device:TPU:0, one launch (start us, length us, event | category | flops | bytes accessed | tf_op | source)
XLA Modules:
  0.0 43.5 jit_solution(8816655469890505016)
XLA Ops:
  0.0 0.5 %collective-permute-start.3 = (bf16[1536,1024]{1,0:T(8,128)(2,1)}, bf16[1536,1024]{1,0:T(8,128)(2,1)S(1)}, u32[]{:S(2)}, u32[]{:S(2)}) collective-permute-start(bf16[1536,1024]{1,0:T(8,128)(2,1)} %head_ref.1), channel_id=1, source_target_pairs={{0,1},{1,0},{2,3},{3,2},{4,5},{5,4},{6,7},{7,6},{8,9},{9,8},{10,11... | collective-permute-start | bytes 9437192 | tf_op jit(solution)/shard_map/ppermute | solution.py:374
  0.5 1.0 %constant_dynamic-slice_fusion = bf16[144,1536]{1,0:T(8,128)(2,1)S(1)} fusion(bf16[256,1536]{1,0:T(8,128)(2,1)} %acts_ref.1, s32[]{:T(128)S(6)} %select_n.11), kind=kLoop, calls=%fused_computation.1 | loop fusion | bytes 884740 | tf_op jit(solution)/shard_map/dynamic_slice | solution.py:372
  1.5 4.4 %collective-permute-start = (bf16[144,1536]{1,0:T(8,128)(2,1)S(1)}, bf16[144,1536]{1,0:T(8,128)(2,1)S(1)}, u32[]{:S(2)}, u32[]{:S(2)}) collective-permute-start(bf16[144,1536]{1,0:T(8,128)(2,1)S(1)} %constant_dynamic-slice_fusion), channel_id=1, source_target_pairs={{0,4},{2,6},{4,8},{5,1},{6,10},{7,3},{8,12},{9,5},{10,14},{11,7},{... | collective-permute-start | bytes 1327112 | tf_op jit(solution)/shard_map/ppermute | solution.py:373
  6.0 0.0 slice-start
  6.0 0.0 slice-start.2
  6.0 0.0 copy-start.7
  6.0 0.0 copy-start.3
  6.0 0.0 slice-start.1
  6.0 0.0 slice-start.3
  6.0 0.0 copy-start
  6.0 0.0 copy-start.1
  6.1 0.0 copy-start.2
  6.1 0.0 copy-start.4
  6.1 0.0 copy-start.5
  6.1 0.0 copy-start.6
  6.1 0.8 %pack_lists.1 = s32[8,8,128]{2,1,0:T(8,128)S(1)} custom-call(s32[1,16]{1,0:T(1,128)} %bitcast.10, s32[16]{0:T(128)} %offsets_ref.1, s32[16]{0:T(128)} %codes_ref.1), custom_call_target="tpu_custom_call" | custom-call | flops 20000000000 | bytes 40000 | tf_op jit(solution)/shard_map/pack_lists/pallas_call | solution.py:329
  7.0 11.6 %all_to_all.10.desc_ref = s32[8,8,128]{2,1,0:T(8,128)S(1)} all-to-all(s32[8,8,128]{2,1,0:T(8,128)S(1)} %pack_lists.1), channel_id=1, replica_groups=mesh['seq'=8,'rep'=4] {'seq'}, dimensions={0} | all-to-all | bytes 65536 | tf_op jit(solution)/shard_map/all_to_all | solution.py:376
  18.6 0.0 collective-permute-done.halo_ref
  18.6 0.0 collective-permute-start.1
  18.6 0.5 %collective-permute-start.2 = (bf16[1024]{0:T(1024)(128)(2,1)S(1)}, bf16[1024]{0:T(1024)(128)(2,1)S(1)}, u32[]{:S(2)}, u32[]{:S(2)}) collective-permute-start(bf16[1024]{0:T(1024)(128)(2,1)S(1)} %copy-done.7), channel_id=1, source_target_pairs={{0,1},{1,0},{2,3},{3,2},{4,5},{5,4},{6,7},{7,6},{8,9},{9,8},{10,11... | collective-permute-start | bytes 6152 | tf_op jit(solution)/shard_map/ppermute | solution.py:375
  19.1 1.0 %slot_table.1 = (s32[16,128]{1,0:T(8,128)S(1)}, s32[8,128]{1,0:T(8,128)S(1)}, bf16[400,1536]{1,0:T(8,128)(2,1)S(1)}) custom-call(s32[8,8,128]{2,1,0:T(8,128)S(1)} %all_to_all.10.desc_ref, bf16[256,1536]{1,0:T(8,128)(2,1)S(1)} %copy-done.3, bf16[144,1536]{1,0:T(8,128)(2,1)S(1)} %collective-permute-done.halo_ref), custom_call_target="tpu_custom_call" | custom-call | flops 491520000 | bytes 2000000 | tf_op jit(solution)/shard_map/slot_table/pallas_call | solution.py:97
  20.1 0.3 collective-permute-done.2.pair_bias_ref
  20.4 0.0 collective-permute-done.1.pair_ref
  20.4 0.0 collective-permute-done.3.pair_head_ref
  20.4 0.0 slice-done.2
  20.4 0.0 slice-done.1
  20.4 0.0 slice-done.3
  20.4 0.0 copy-done
  20.5 10.0 %trunk_and_head.1 = f32[256,128]{1,0:T(8,128)} custom-call(s32[16,128]{1,0:T(8,128)S(1)} %get-tuple-element.13.slots_ref, bf16[400,1536]{1,0:T(8,128)(2,1)S(1)} %get-tuple-element.14.early_ref, bf16[144,1536]{1,0:T(8,128)(2,1)S(1)} %collective-permute-done.1.pair_ref, bf16[4,1536]{1,0:T(4,128)(2,1)S(1)} %copy-done.4, bf16[1536]{0:T(1024)(128)(2,1)S(1)} %copy-done.5, ...), custom_call_target="tpu_custom_call" | custom-call | flops 6341787648 | bytes 29360128 | tf_op jit(solution)/shard_map/trunk_and_head/pallas_call | solution.py:276
  30.5 4.2 %all-to-all-start.1 = ((f32[16,16,128]{2,1,0:T(8,128)}), f32[16,16,128]{2,1,0:T(8,128)S(1)}, u32[]{:S(2)}, u32[]{:S(2)}) async-start(f32[16,16,128]{2,1,0:T(8,128)} %bitcast.2), calls=%async_computation.1 | async-start | bytes 262144 | tf_op jit(solution)/shard_map/all_to_all | solution.py:397
  34.6 7.7 %all-to-all-done.1 = f32[16,16,128]{2,1,0:T(8,128)S(1)} async-done(((f32[16,16,128]{2,1,0:T(8,128)}), f32[16,16,128]{2,1,0:T(8,128)S(1)}, u32[]{:S(2)}, u32[]{:S(2)}) %all-to-all-start.1) | async-done | bytes 131104 | tf_op jit(solution)/shard_map/all_to_all | solution.py:397
  42.3 1.2 %pick_scores.1 = f32[16,1024]{1,0:T(8,128)} custom-call(s32[128]{0:T(128)S(1)} %slice_bitcast_fusion.places_ref, f32[256,128]{1,0:T(8,128)S(1)} %bitcast.9), custom_call_target="tpu_custom_call" | custom-call | tf_op jit(solution)/shard_map/pick_scores/pallas_call | solution.py:406
  (11 shorter events, 0.0 us)
Async XLA Ops:
  0.0 20.4 %collective-permute-start.3 = (bf16[1536,1024]{1,0:T(8,128)(2,1)}, bf16[1536,1024]{1,0:T(8,128)(2,1)S(1)}, u32[]{:S(2)}, u32[]{:S(2)}) collective-permute-start(bf16[1536,1024]{1,0:T(8,128)(2,1)} %head_ref.1), channel_id=1, source_target_pairs={{0,1},{1,0},{2,3},{3,2},{4,5},{5,4},{6,7},{7,6},{8,9},{9,8},{10,11... | collective-permute-start | bytes 9437192 | tf_op jit(solution)/shard_map/ppermute | solution.py:374
  1.5 17.1 %collective-permute-start = (bf16[144,1536]{1,0:T(8,128)(2,1)S(1)}, bf16[144,1536]{1,0:T(8,128)(2,1)S(1)}, u32[]{:S(2)}, u32[]{:S(2)}) collective-permute-start(bf16[144,1536]{1,0:T(8,128)(2,1)S(1)} %constant_dynamic-slice_fusion), channel_id=1, source_target_pairs={{0,4},{2,6},{4,8},{5,1},{6,10},{7,3},{8,12},{9,5},{10,14},{11,7},{... | collective-permute-start | bytes 1327112 | tf_op jit(solution)/shard_map/ppermute | solution.py:373
  6.0 14.4 %slice-start = ((s8[7077888]{0:T(1024)(128)(4,1)}), s8[4194304]{0:T(1024)(128)(4,1)S(1)}, s32[]{:S(2)}) async-start(s8[7077888]{0:T(1024)(128)(4,1)} %bitcast.5), calls=%async_computation.2 | async-start | bytes 8388608
  6.0 14.4 %slice-start.2 = ((s8[7077888]{0:T(1024)(128)(4,1)}), s8[4194304]{0:T(1024)(128)(4,1)S(1)}, s32[]{:S(2)}) async-start(s8[7077888]{0:T(1024)(128)(4,1)} %bitcast.7), calls=%async_computation.4 | async-start | bytes 8388608
  6.0 12.6 %copy-start.7 = (bf16[1024]{0:T(1024)(128)(2,1)S(1)}, bf16[1024]{0:T(1024)(128)(2,1)}, u32[]{:S(2)}) copy-start(bf16[1024]{0:T(1024)(128)(2,1)} %bias_ref.1) | copy-start | bytes 6148
  6.0 13.1 %copy-start.3 = (bf16[256,1536]{1,0:T(8,128)(2,1)S(1)}, bf16[256,1536]{1,0:T(8,128)(2,1)}, u32[]{:S(2)}) copy-start(bf16[256,1536]{1,0:T(8,128)(2,1)} %acts_ref.1) | copy-start | bytes 2359300
  6.0 14.4 %slice-start.1 = ((s8[7077888]{0:T(1024)(128)(4,1)}), s8[2883584]{0:T(1024)(128)(4,1)S(1)}, s32[]{:S(2)}) async-start(s8[7077888]{0:T(1024)(128)(4,1)} %bitcast.5), calls=%async_computation.3 | async-start | bytes 5767168
  6.0 14.4 %slice-start.3 = ((s8[7077888]{0:T(1024)(128)(4,1)}), s8[2883584]{0:T(1024)(128)(4,1)S(1)}, s32[]{:S(2)}) async-start(s8[7077888]{0:T(1024)(128)(4,1)} %bitcast.7), calls=%async_computation.5 | async-start | bytes 5767168
  6.0 14.4 %copy-start = (bf16[1536,1024]{1,0:T(8,128)(2,1)S(1)}, bf16[1536,1024]{1,0:T(8,128)(2,1)}, u32[]{:S(2)}) copy-start(bf16[1536,1024]{1,0:T(8,128)(2,1)} %head_ref.1) | copy-start | bytes 9437188
  6.0 14.4 %copy-start.1 = (bf16[768,1536]{1,0:T(8,128)(2,1)S(1)}, bf16[768,1536]{1,0:T(8,128)(2,1)}, u32[]{:S(2)}) copy-start(bf16[768,1536]{1,0:T(8,128)(2,1)} %proj1_ref.1) | copy-start | bytes 7077892
  6.1 14.4 %copy-start.2 = (bf16[768,1536]{1,0:T(8,128)(2,1)S(1)}, bf16[768,1536]{1,0:T(8,128)(2,1)}, u32[]{:S(2)}) copy-start(bf16[768,1536]{1,0:T(8,128)(2,1)} %proj2_ref.1) | copy-start | bytes 7077892
  6.1 14.4 %copy-start.4 = (bf16[4,1536]{1,0:T(4,128)(2,1)S(1)}, bf16[4,1536]{1,0:T(4,128)(2,1)}, u32[]{:S(2)}) copy-start(bf16[4,1536]{1,0:T(4,128)(2,1)} %delta_ref.1) | copy-start | bytes 36868
  6.1 14.4 %copy-start.5 = (bf16[1536]{0:T(1024)(128)(2,1)S(1)}, bf16[1536]{0:T(1024)(128)(2,1)}, u32[]{:S(2)}) copy-start(bf16[1536]{0:T(1024)(128)(2,1)} %gain1_ref.1) | copy-start | bytes 9220
  6.1 14.4 %copy-start.6 = (bf16[1536]{0:T(1024)(128)(2,1)S(1)}, bf16[1536]{0:T(1024)(128)(2,1)}, u32[]{:S(2)}) copy-start(bf16[1536]{0:T(1024)(128)(2,1)} %gain2_ref.1) | copy-start | bytes 9220
  18.6 1.8 %collective-permute-start.1 = (bf16[144,1536]{1,0:T(8,128)(2,1)S(1)}, bf16[144,1536]{1,0:T(8,128)(2,1)S(1)}, u32[]{:S(2)}, u32[]{:S(2)}) collective-permute-start(bf16[144,1536]{1,0:T(8,128)(2,1)S(1)} %collective-permute-done.halo_ref), channel_id=1, source_target_pairs={{0,1},{1,0},{2,3},{3,2},{4,5},{5,4},{6,7},{7,6},{8,9},{9,8},{10,11... | collective-permute-start | bytes 1327112 | tf_op jit(solution)/shard_map/ppermute | solution.py:378
  18.6 1.8 %collective-permute-start.2 = (bf16[1024]{0:T(1024)(128)(2,1)S(1)}, bf16[1024]{0:T(1024)(128)(2,1)S(1)}, u32[]{:S(2)}, u32[]{:S(2)}) collective-permute-start(bf16[1024]{0:T(1024)(128)(2,1)S(1)} %copy-done.7), channel_id=1, source_target_pairs={{0,1},{1,0},{2,3},{3,2},{4,5},{5,4},{6,7},{7,6},{8,9},{9,8},{10,11... | collective-permute-start | bytes 6152 | tf_op jit(solution)/shard_map/ppermute | solution.py:375
  30.5 11.8 %all-to-all-start.1 = ((f32[16,16,128]{2,1,0:T(8,128)}), f32[16,16,128]{2,1,0:T(8,128)S(1)}, u32[]{:S(2)}, u32[]{:S(2)}) async-start(f32[16,16,128]{2,1,0:T(8,128)} %bitcast.2), calls=%async_computation.1 | async-start | bytes 262144 | tf_op jit(solution)/shard_map/all_to_all | solution.py:397

commit v3 on v2

--- a/solution.py
+++ b/solution.py
@@ -138,6 +138,7 @@
     h1,
     n2,
     h2,
+    packed,
 ):
     S = slots
     C = early_ref.shape[1]
@@ -258,7 +259,8 @@
             per = tracks // 128
             for t in range(NT // 128):
                 start = block + n * (NT // 128) + t
-                out_ref[pl.ds(start, S, stride=per), :] = score[:, t * 128 : (t + 1) * 128]
+                packed[pl.ds(start, S, stride=per), :] = score[:, t * 128 : (t + 1) * 128]
+    out_ref[...] = packed[...].astype(BF16)
 
 
 def trunk_and_head(table, early, pair, delta, gain1, gain2, bias, pair_bias, weights, width, genome):
@@ -275,7 +277,7 @@
     ]
     return pl.pallas_call(
         functools.partial(trunk_kernel, S, width, genome),
-        out_shape=jax.ShapeDtypeStruct((2 * S * tracks // 128, 128), F32),
+        out_shape=jax.ShapeDtypeStruct((2 * S * tracks // 128, 128), BF16),
         in_specs=[vm] * len(operands),
         out_specs=vm,
         scratch_shapes=[
@@ -286,6 +288,7 @@
             pltpu.VMEM((18 * S, C), BF16),
             pltpu.VMEM((18 * S, C), BF16),
             pltpu.VMEM((18 * S, C), BF16),
+            pltpu.VMEM((2 * S * tracks // 128, 128), F32),
         ],
         compiler_params=pltpu.CompilerParams(vmem_limit_bytes=12 * 1024 * 1024),
         cost_estimate=pl.CostEstimate(
@@ -295,12 +298,13 @@
     )(*operands)
 
 
-def return_kernel(places_ref, got_ref, out_ref, tiles):
+def return_kernel(places_ref, got_ref, out_ref, wide, tiles):
+    wide[...] = got_ref[...].astype(F32)
     count, tracks = out_ref.shape
     per = tracks // 128
     for v in range(count):
         row = pl.multiple_of(places_ref[v], 8)
-        tiles[v * per : (v + 1) * per, :] = got_ref[pl.ds(row, per), :]
+        tiles[v * per : (v + 1) * per, :] = wide[pl.ds(row, per), :]
     for t in range(per):
         out_ref[:, t * 128 : (t + 1) * 128] = tiles[pl.ds(t, count, stride=per), :]
 
@@ -408,7 +412,7 @@
         out_shape=jax.ShapeDtypeStruct((vcount, tracks), F32),
         in_specs=[pl.BlockSpec(memory_space=pltpu.SMEM), pl.BlockSpec(memory_space=pltpu.VMEM)],
         out_specs=pl.BlockSpec(memory_space=pltpu.VMEM),
-        scratch_shapes=[pltpu.VMEM((vcount * per, 128), F32)],
+        scratch_shapes=[pltpu.VMEM(got.shape, F32), pltpu.VMEM((vcount * per, 128), F32)],
         compiler_params=pltpu.CompilerParams(vmem_limit_bytes=2 * 1024 * 1024),
         name="pick_scores",
     )(places[0], got)

time: 43.8 us -> 42.8 us (0.977)
  waiting for transfers between devices: 7.92 us -> 7.01 us
    all_to_all x1, waiting for transfers between devices: 7.66 us -> 6.75 us  [per_device(): lax.all_to_all(scores.reshape(2 * n_seq, half_cap * per, 128), ('seq', 'r...]
where the time goes in v3:
time: 42.8 us; the launch traced here: 42.6 us
  Pallas kernels  13.1 us (31%)
  blocking collectives  11.6 us (27%)
  starting transfers between devices  9.57 us (22%)
  waiting for transfers between devices  7.01 us (16%)
  local copies, waits for them, and re-layouts  1.12 us (3%)
    all_to_all x1, blocking collectives, per_device(): lax.all_to_all(fields, 'seq', split_axis=0, concat_axis=0, tiled=True)  11.6 us
    pallas_call x1, Pallas kernels, trunk_and_head(): pl.pallas_call(functools.partial(trunk_kernel, S, width, genome), out_sha...  9.98 us
    all_to_all x1, waiting for transfers between devices, per_device(): lax.all_to_all(scores.reshape(2 * n_seq, half_cap * per, 128), ('seq', 'r...  6.75 us
    ppermute x1, starting transfers between devices, per_device(): halo = lax.ppermute(edge, ('seq', 'rep'), edges)  4.45 us
    all_to_all x1, starting transfers between devices, per_device(): lax.all_to_all(scores.reshape(2 * n_seq, half_cap * per, 128), ('seq', 'r...  4.16 us
    pallas_call x1, Pallas kernels, per_device(): pl.pallas_call(return_kernel, out_shape=jax.ShapeDtypeStruct((vcount, tra...  1.2 us
    dynamic_slice x1, local copies, waits for them, and re-layouts, per_device(): lax.dynamic_slice_in_dim(reference_acts, (1 - core) * (width - REACH), RE...  1.04 us
    pallas_call x1, Pallas kernels, slot_table(): pl.pallas_call(functools.partial(slot_kernel, half_cap, per), out_shape=(...  1.02 us
  transfers between devices with their start and end apart: 5, of which 2 were waited for; matrix products, arithmetic and copies ran while one was open for 2% of the time, Pallas kernels for 4%

profile of v3, /device:TPU:0, one launch (start us, length us, event | category | flops | bytes accessed | tf_op | source)
XLA Modules:
  0.0 42.6 jit_solution(17756187799592650318)
XLA Ops:
  0.0 0.5 %collective-permute-start.3 = (bf16[1536,1024]{1,0:T(8,128)(2,1)}, bf16[1536,1024]{1,0:T(8,128)(2,1)S(1)}, u32[]{:S(2)}, u32[]{:S(2)}) collective-permute-start(bf16[1536,1024]{1,0:T(8,128)(2,1)} %head_ref.1), channel_id=1, source_target_pairs={{0,1},{1,0},{2,3},{3,2},{4,5},{5,4},{6,7},{7,6},{8,9},{9,8},{10,11... | collective-permute-start | bytes 9437192 | tf_op jit(solution)/shard_map/ppermute | solution.py:378
  0.5 1.0 %constant_dynamic-slice_fusion = bf16[144,1536]{1,0:T(8,128)(2,1)S(1)} fusion(bf16[256,1536]{1,0:T(8,128)(2,1)} %acts_ref.1, s32[]{:T(128)S(6)} %select_n.11), kind=kLoop, calls=%fused_computation.1 | loop fusion | bytes 884740 | tf_op jit(solution)/shard_map/dynamic_slice | solution.py:376
  1.5 4.4 %collective-permute-start = (bf16[144,1536]{1,0:T(8,128)(2,1)S(1)}, bf16[144,1536]{1,0:T(8,128)(2,1)S(1)}, u32[]{:S(2)}, u32[]{:S(2)}) collective-permute-start(bf16[144,1536]{1,0:T(8,128)(2,1)S(1)} %constant_dynamic-slice_fusion), channel_id=1, source_target_pairs={{0,4},{2,6},{4,8},{5,1},{6,10},{7,3},{8,12},{9,5},{10,14},{11,7},{... | collective-permute-start | bytes 1327112 | tf_op jit(solution)/shard_map/ppermute | solution.py:377
  6.0 0.0 slice-start
  6.0 0.0 slice-start.2
  6.0 0.0 copy-start.7
  6.0 0.0 copy-start.3
  6.0 0.0 slice-start.1
  6.0 0.0 slice-start.3
  6.0 0.0 copy-start
  6.0 0.0 copy-start.1
  6.1 0.0 copy-start.2
  6.1 0.0 copy-start.4
  6.1 0.0 copy-start.5
  6.1 0.0 copy-start.6
  6.1 0.8 %pack_lists.1 = s32[8,8,128]{2,1,0:T(8,128)S(1)} custom-call(s32[1,16]{1,0:T(1,128)} %bitcast.10, s32[16]{0:T(128)} %offsets_ref.1, s32[16]{0:T(128)} %codes_ref.1), custom_call_target="tpu_custom_call" | custom-call | flops 20000000000 | bytes 40000 | tf_op jit(solution)/shard_map/pack_lists/pallas_call | solution.py:333
  7.0 11.6 %all_to_all.10.desc_ref = s32[8,8,128]{2,1,0:T(8,128)S(1)} all-to-all(s32[8,8,128]{2,1,0:T(8,128)S(1)} %pack_lists.1), channel_id=1, replica_groups=mesh['seq'=8,'rep'=4] {'seq'}, dimensions={0} | all-to-all | bytes 65536 | tf_op jit(solution)/shard_map/all_to_all | solution.py:380
  18.6 0.0 collective-permute-done.halo_ref
  18.6 0.0 collective-permute-start.1
  18.6 0.5 %collective-permute-start.2 = (bf16[1024]{0:T(1024)(128)(2,1)S(1)}, bf16[1024]{0:T(1024)(128)(2,1)S(1)}, u32[]{:S(2)}, u32[]{:S(2)}) collective-permute-start(bf16[1024]{0:T(1024)(128)(2,1)S(1)} %copy-done.7), channel_id=1, source_target_pairs={{0,1},{1,0},{2,3},{3,2},{4,5},{5,4},{6,7},{7,6},{8,9},{9,8},{10,11... | collective-permute-start | bytes 6152 | tf_op jit(solution)/shard_map/ppermute | solution.py:379
  19.1 1.0 %slot_table.1 = (s32[16,128]{1,0:T(8,128)S(1)}, s32[8,128]{1,0:T(8,128)S(1)}, bf16[400,1536]{1,0:T(8,128)(2,1)S(1)}) custom-call(s32[8,8,128]{2,1,0:T(8,128)S(1)} %all_to_all.10.desc_ref, bf16[256,1536]{1,0:T(8,128)(2,1)S(1)} %copy-done.3, bf16[144,1536]{1,0:T(8,128)(2,1)S(1)} %collective-permute-done.halo_ref), custom_call_target="tpu_custom_call" | custom-call | flops 491520000 | bytes 2000000 | tf_op jit(solution)/shard_map/slot_table/pallas_call | solution.py:97
  20.1 0.3 collective-permute-done.2.pair_bias_ref
  20.4 0.0 collective-permute-done.1.pair_ref
  20.4 0.0 collective-permute-done.3.pair_head_ref
  20.4 0.0 slice-done.2
  20.4 0.0 slice-done.1
  20.4 0.0 slice-done.3
  20.4 0.0 copy-done
  20.5 10.0 %trunk_and_head.1 = bf16[256,128]{1,0:T(8,128)(2,1)} custom-call(s32[16,128]{1,0:T(8,128)S(1)} %get-tuple-element.13.slots_ref, bf16[400,1536]{1,0:T(8,128)(2,1)S(1)} %get-tuple-element.14.early_ref, bf16[144,1536]{1,0:T(8,128)(2,1)S(1)} %collective-permute-done.1.pair_ref, bf16[4,1536]{1,0:T(4,128)(2,1)S(1)} %copy-done.4, bf16[1536]{0:T(1024)(128)(2,1)S(1)} %copy-done.5, ...), custom_call_target="tpu_custom_call" | custom-call | flops 6341787648 | bytes 29360128 | tf_op jit(solution)/shard_map/trunk_and_head/pallas_call | solution.py:278
  30.5 4.2 %all-to-all-start.1 = ((bf16[16,16,128]{2,1,0:T(8,128)(2,1)}), bf16[16,16,128]{2,1,0:T(8,128)(2,1)S(1)}, u32[]{:S(2)}, u32[]{:S(2)}) async-start(bf16[16,16,128]{2,1,0:T(8,128)(2,1)} %bitcast.2), calls=%async_computation.1 | async-start | bytes 131072 | tf_op jit(solution)/shard_map/all_to_all | solution.py:401
  34.6 6.8 %all-to-all-done.1 = bf16[16,16,128]{2,1,0:T(8,128)(2,1)S(1)} async-done(((bf16[16,16,128]{2,1,0:T(8,128)(2,1)}), bf16[16,16,128]{2,1,0:T(8,128)(2,1)S(1)}, u32[]{:S(2)}, u32[]{:S(2)}) %all-to-all-start.1) | async-done | bytes 65568 | tf_op jit(solution)/shard_map/all_to_all | solution.py:401
  41.4 1.2 %pick_scores.1 = f32[16,1024]{1,0:T(8,128)} custom-call(s32[128]{0:T(128)S(1)} %slice_bitcast_fusion.places_ref, bf16[256,128]{1,0:T(8,128)(2,1)S(1)} %bitcast.9), custom_call_target="tpu_custom_call" | custom-call | tf_op jit(solution)/shard_map/pick_scores/pallas_call | solution.py:410
  (11 shorter events, 0.0 us)
Async XLA Ops:
  0.0 20.4 %collective-permute-start.3 = (bf16[1536,1024]{1,0:T(8,128)(2,1)}, bf16[1536,1024]{1,0:T(8,128)(2,1)S(1)}, u32[]{:S(2)}, u32[]{:S(2)}) collective-permute-start(bf16[1536,1024]{1,0:T(8,128)(2,1)} %head_ref.1), channel_id=1, source_target_pairs={{0,1},{1,0},{2,3},{3,2},{4,5},{5,4},{6,7},{7,6},{8,9},{9,8},{10,11... | collective-permute-start | bytes 9437192 | tf_op jit(solution)/shard_map/ppermute | solution.py:378
  1.5 17.1 %collective-permute-start = (bf16[144,1536]{1,0:T(8,128)(2,1)S(1)}, bf16[144,1536]{1,0:T(8,128)(2,1)S(1)}, u32[]{:S(2)}, u32[]{:S(2)}) collective-permute-start(bf16[144,1536]{1,0:T(8,128)(2,1)S(1)} %constant_dynamic-slice_fusion), channel_id=1, source_target_pairs={{0,4},{2,6},{4,8},{5,1},{6,10},{7,3},{8,12},{9,5},{10,14},{11,7},{... | collective-permute-start | bytes 1327112 | tf_op jit(solution)/shard_map/ppermute | solution.py:377
  6.0 14.4 %slice-start = ((s8[7077888]{0:T(1024)(128)(4,1)}), s8[4194304]{0:T(1024)(128)(4,1)S(1)}, s32[]{:S(2)}) async-start(s8[7077888]{0:T(1024)(128)(4,1)} %bitcast.5), calls=%async_computation.2 | async-start | bytes 8388608
  6.0 14.4 %slice-start.2 = ((s8[7077888]{0:T(1024)(128)(4,1)}), s8[4194304]{0:T(1024)(128)(4,1)S(1)}, s32[]{:S(2)}) async-start(s8[7077888]{0:T(1024)(128)(4,1)} %bitcast.7), calls=%async_computation.4 | async-start | bytes 8388608
  6.0 12.6 %copy-start.7 = (bf16[1024]{0:T(1024)(128)(2,1)S(1)}, bf16[1024]{0:T(1024)(128)(2,1)}, u32[]{:S(2)}) copy-start(bf16[1024]{0:T(1024)(128)(2,1)} %bias_ref.1) | copy-start | bytes 6148
  6.0 13.1 %copy-start.3 = (bf16[256,1536]{1,0:T(8,128)(2,1)S(1)}, bf16[256,1536]{1,0:T(8,128)(2,1)}, u32[]{:S(2)}) copy-start(bf16[256,1536]{1,0:T(8,128)(2,1)} %acts_ref.1) | copy-start | bytes 2359300
  6.0 14.4 %slice-start.1 = ((s8[7077888]{0:T(1024)(128)(4,1)}), s8[2883584]{0:T(1024)(128)(4,1)S(1)}, s32[]{:S(2)}) async-start(s8[7077888]{0:T(1024)(128)(4,1)} %bitcast.5), calls=%async_computation.3 | async-start | bytes 5767168
  6.0 14.4 %slice-start.3 = ((s8[7077888]{0:T(1024)(128)(4,1)}), s8[2883584]{0:T(1024)(128)(4,1)S(1)}, s32[]{:S(2)}) async-start(s8[7077888]{0:T(1024)(128)(4,1)} %bitcast.7), calls=%async_computation.5 | async-start | bytes 5767168
  6.0 14.4 %copy-start = (bf16[1536,1024]{1,0:T(8,128)(2,1)S(1)}, bf16[1536,1024]{1,0:T(8,128)(2,1)}, u32[]{:S(2)}) copy-start(bf16[1536,1024]{1,0:T(8,128)(2,1)} %head_ref.1) | copy-start | bytes 9437188
  6.0 14.4 %copy-start.1 = (bf16[768,1536]{1,0:T(8,128)(2,1)S(1)}, bf16[768,1536]{1,0:T(8,128)(2,1)}, u32[]{:S(2)}) copy-start(bf16[768,1536]{1,0:T(8,128)(2,1)} %proj1_ref.1) | copy-start | bytes 7077892
  6.1 14.4 %copy-start.2 = (bf16[768,1536]{1,0:T(8,128)(2,1)S(1)}, bf16[768,1536]{1,0:T(8,128)(2,1)}, u32[]{:S(2)}) copy-start(bf16[768,1536]{1,0:T(8,128)(2,1)} %proj2_ref.1) | copy-start | bytes 7077892
  6.1 14.4 %copy-start.4 = (bf16[4,1536]{1,0:T(4,128)(2,1)S(1)}, bf16[4,1536]{1,0:T(4,128)(2,1)}, u32[]{:S(2)}) copy-start(bf16[4,1536]{1,0:T(4,128)(2,1)} %delta_ref.1) | copy-start | bytes 36868
  6.1 14.4 %copy-start.5 = (bf16[1536]{0:T(1024)(128)(2,1)S(1)}, bf16[1536]{0:T(1024)(128)(2,1)}, u32[]{:S(2)}) copy-start(bf16[1536]{0:T(1024)(128)(2,1)} %gain1_ref.1) | copy-start | bytes 9220
  6.1 14.4 %copy-start.6 = (bf16[1536]{0:T(1024)(128)(2,1)S(1)}, bf16[1536]{0:T(1024)(128)(2,1)}, u32[]{:S(2)}) copy-start(bf16[1536]{0:T(1024)(128)(2,1)} %gain2_ref.1) | copy-start | bytes 9220
  18.6 1.8 %collective-permute-start.1 = (bf16[144,1536]{1,0:T(8,128)(2,1)S(1)}, bf16[144,1536]{1,0:T(8,128)(2,1)S(1)}, u32[]{:S(2)}, u32[]{:S(2)}) collective-permute-start(bf16[144,1536]{1,0:T(8,128)(2,1)S(1)} %collective-permute-done.halo_ref), channel_id=1, source_target_pairs={{0,1},{1,0},{2,3},{3,2},{4,5},{5,4},{6,7},{7,6},{8,9},{9,8},{10,11... | collective-permute-start | bytes 1327112 | tf_op jit(solution)/shard_map/ppermute | solution.py:382
  18.6 1.8 %collective-permute-start.2 = (bf16[1024]{0:T(1024)(128)(2,1)S(1)}, bf16[1024]{0:T(1024)(128)(2,1)S(1)}, u32[]{:S(2)}, u32[]{:S(2)}) collective-permute-start(bf16[1024]{0:T(1024)(128)(2,1)S(1)} %copy-done.7), channel_id=1, source_target_pairs={{0,1},{1,0},{2,3},{3,2},{4,5},{5,4},{6,7},{7,6},{8,9},{9,8},{10,11... | collective-permute-start | bytes 6152 | tf_op jit(solution)/shard_map/ppermute | solution.py:379
  30.5 10.9 %all-to-all-start.1 = ((bf16[16,16,128]{2,1,0:T(8,128)(2,1)}), bf16[16,16,128]{2,1,0:T(8,128)(2,1)S(1)}, u32[]{:S(2)}, u32[]{:S(2)}) async-start(bf16[16,16,128]{2,1,0:T(8,128)(2,1)} %bitcast.2), calls=%async_computation.1 | async-start | bytes 131072 | tf_op jit(solution)/shard_map/all_to_all | solution.py:401

commit v4 on v3

--- a/solution.py
+++ b/solution.py
@@ -309,40 +309,64 @@
         out_ref[:, t * 128 : (t + 1) * 128] = tiles[pl.ds(t, count, stride=per), :]
 
 
-def pack_kernel(owners_ref, offsets_ref, codes_ref, out_ref, rows, sem):
-    lists = out_ref.shape[0]
+def first_kernel(acts_ref, owners_ref, offsets_ref, codes_ref, edge_ref, out_ref, rows, sem):
+    core = lax.rem(lax.axis_index("rep"), 2)
     count = owners_ref.shape[1]
-    copies = [
+    reach = edge_ref.shape[0]
+    begin = pl.multiple_of((1 - core) * (acts_ref.shape[0] - reach), 16)
+    copies = [pltpu.make_async_copy(acts_ref.at[pl.ds(begin, reach)], edge_ref, sem.at[3])]
+    copies += [
         pltpu.make_async_copy(ref, row, sem.at[i])
         for i, (ref, row) in enumerate(zip((owners_ref, offsets_ref, codes_ref), rows))
     ]
     for copy in copies:
         copy.start()
     out_ref[...] = jnp.full(out_ref.shape, -1, jnp.int32)
-    for copy in copies:
+    for copy in copies[1:]:
         copy.wait()
     for f in range(3):
-        row = rows[f][...].reshape(1, count)
-        for s in range(lists):
-            out_ref[s, f : f + 1, 0:count] = row
-
-
-def pack_lists(owner, offsets, codes, lists):
+        out_ref[f : f + 1, 0:count] = rows[f][...].reshape(1, count)
+    copies[0].wait()
+
+
+def edge_and_list(acts, owner, offsets, codes):
     hbm = pl.BlockSpec(memory_space=pltpu.HBM)
-    args = [pltpu.with_memory_space_constraint(a, pltpu.HBM) for a in (owner, offsets, codes)]
+    vm = pl.BlockSpec(memory_space=pltpu.VMEM)
+    args = [pltpu.with_memory_space_constraint(a, pltpu.HBM) for a in (acts, owner, offsets, codes)]
     return pl.pallas_call(
-        pack_kernel,
+        first_kernel,
+        out_shape=(
+            jax.ShapeDtypeStruct((REACH, acts.shape[1]), BF16),
+            jax.ShapeDtypeStruct((8, 128), jnp.int32),
+        ),
+        in_specs=[hbm, hbm, hbm, hbm],
+        out_specs=(vm, vm),
+        scratch_shapes=[
+            [pltpu.VMEM(a.shape, jnp.int32) for a in args[1:]],
+            pltpu.SemaphoreType.DMA((4,)),
+        ],
+        compiler_params=pltpu.CompilerParams(vmem_limit_bytes=2 * 1024 * 1024),
+        cost_estimate=pl.CostEstimate(flops=1_000, bytes_accessed=900_000, transcendentals=0),
+        name="edge_and_list",
+    )(*args)
+
+
+def spread_kernel(list_ref, out_ref):
+    for s in range(out_ref.shape[0]):
+        out_ref[s] = list_ref[...]
+
+
+def spread(fields, lists):
+    vm = pl.BlockSpec(memory_space=pltpu.VMEM)
+    return pl.pallas_call(
+        spread_kernel,
         out_shape=jax.ShapeDtypeStruct((lists, 8, 128), jnp.int32),
-        in_specs=[hbm, hbm, hbm],
-        out_specs=pl.BlockSpec(memory_space=pltpu.VMEM),
-        scratch_shapes=[
-            [pltpu.VMEM(a.shape, jnp.int32) for a in args],
-            pltpu.SemaphoreType.DMA((3,)),
-        ],
+        in_specs=[vm],
+        out_specs=vm,
         compiler_params=pltpu.CompilerParams(vmem_limit_bytes=1024 * 1024),
         cost_estimate=pl.CostEstimate(flops=20_000_000_000, bytes_accessed=40_000, transcendentals=0),
-        name="pack_lists",
-    )(*args)
+        name="spread_list",
+    )(pltpu.with_memory_space_constraint(fields, pltpu.VMEM))
 
 
 def per_device(
@@ -371,11 +395,11 @@
     steps = [(i, r, i + 1 - 2 * (r % 2)) for i in range(n_seq) for r in range(n_rep)]
     edges = [(i * n_rep + r, j * n_rep + r) for i, r, j in steps if 0 <= j < n_seq]
 
-    fields = pack_lists(owners.reshape(1, vcount), offsets, codes, n_seq)
-    core = lax.axis_index("rep") % 2
-    edge = lax.dynamic_slice_in_dim(reference_acts, (1 - core) * (width - REACH), REACH, 0)
+    edge, fields = edge_and_list(reference_acts, owners.reshape(1, vcount), offsets, codes)
+    fields = spread(fields, n_seq)
     halo = lax.ppermute(edge, ("seq", "rep"), edges)
-    pair_head = lax.ppermute(head_weight, "rep", swap)
+    late_head, edge = lax.optimization_barrier((head_weight, edge))
+    pair_head = lax.ppermute(late_head, "rep", swap)
     pair_bias = lax.ppermute(head_bias, "rep", swap)
     desc = lax.all_to_all(fields, "seq", split_axis=0, concat_axis=0, tiled=True)
     halo, desc = lax.optimization_barrier((halo, desc))

time: 42.8 us -> 43.2 us (level)
  local copies, waits for them, and re-layouts: 1.12 us -> 0.08 us
  starting transfers between devices: 9.57 us -> 10.5 us
    dynamic_slice x1 -> x0, local copies, waits for them, and re-layouts: 1.04 us -> none  [per_device(): lax.dynamic_slice_in_dim(reference_acts, (1 - core) * (width - REACH), RE...]
    all_to_all x1, starting transfers between devices: 4.16 us -> 4.99 us  [per_device(): lax.all_to_all(scores.reshape(2 * n_seq, half_cap * per, 128), ('seq', 'r...]
    pallas_call x1 -> x2, Pallas kernels: 0.85 us -> 1.05 us  [the longest x1 1.05 us: edge_and_list(): pl.pallas_call(first_kernel, out_shape=(jax.ShapeDtypeStruct((REACH, acts...]
  transfers between devices with their start and end apart: 5 -> 5, of which waited for: 2 -> 2; matrix products, arithmetic and copies ran while one was open for 2% -> 0% of each run, Pallas kernels for 4% -> 2%
where the time goes in v4:
time: 43.2 us; the launch traced here: 42.9 us
  Pallas kernels  13.5 us (31%)
  blocking collectives  11.6 us (27%)
  starting transfers between devices  10.5 us (24%)
  waiting for transfers between devices  7.02 us (16%)
    all_to_all x1, blocking collectives, per_device(): lax.all_to_all(fields, 'seq', split_axis=0, concat_axis=0, tiled=True)  11.6 us
    pallas_call x1, Pallas kernels, trunk_and_head(): pl.pallas_call(functools.partial(trunk_kernel, S, width, genome), out_sha...  10.3 us
    all_to_all x1, waiting for transfers between devices, per_device(): lax.all_to_all(scores.reshape(2 * n_seq, half_cap * per, 128), ('seq', 'r...  6.75 us
    all_to_all x1, starting transfers between devices, per_device(): lax.all_to_all(scores.reshape(2 * n_seq, half_cap * per, 128), ('seq', 'r...  4.99 us
    ppermute x1, starting transfers between devices, per_device(): halo = lax.ppermute(edge, ('seq', 'rep'), edges)  4.46 us
    pallas_call x1, Pallas kernels, per_device(): pl.pallas_call(return_kernel, out_shape=jax.ShapeDtypeStruct((vcount, tra...  1.2 us
    pallas_call x1, Pallas kernels, edge_and_list(): pl.pallas_call(first_kernel, out_shape=(jax.ShapeDtypeStruct((REACH, acts...  1.05 us
    pallas_call x1, Pallas kernels, slot_table(): pl.pallas_call(functools.partial(slot_kernel, half_cap, per), out_shape=(...  1.02 us
  transfers between devices with their start and end apart: 5, of which 2 were waited for; matrix products, arithmetic and copies ran while one was open for 0% of the time, Pallas kernels for 2%

profile of v4, /device:TPU:0, one launch (start us, length us, event | category | flops | bytes accessed | tf_op | source)
XLA Modules:
  0.0 42.9 jit_solution(4770012639946952635)
XLA Ops:
  0.0 1.0 %edge_and_list.1 = (bf16[144,1536]{1,0:T(8,128)(2,1)S(1)}, s32[8,128]{1,0:T(8,128)S(1)}) custom-call(bf16[256,1536]{1,0:T(8,128)(2,1)} %acts_ref.3, s32[1,16]{1,0:T(1,128)} %bitcast.10, s32[16]{0:T(128)} %offsets_ref.1, s32[16]{0:T(128)} %codes_ref.1), custom_call_target="tpu_custom_call" | custom-call | flops 1000 | bytes 900000 | tf_op jit(solution)/shard_map/edge_and_list/pallas_call | solution.py:336
  1.1 0.5 %collective-permute-start.3 = (bf16[1536,1024]{1,0:T(8,128)(2,1)}, bf16[1536,1024]{1,0:T(8,128)(2,1)S(1)}, u32[]{:S(2)}, u32[]{:S(2)}) collective-permute-start(bf16[1536,1024]{1,0:T(8,128)(2,1)} %head_ref.1), channel_id=1, source_target_pairs={{0,1},{1,0},{2,3},{3,2},{4,5},{5,4},{6,7},{7,6},{8,9},{9,8},{10,11... | collective-permute-start | bytes 9437192 | tf_op jit(solution)/shard_map/ppermute | solution.py:402
  1.6 4.5 %collective-permute-start = (bf16[144,1536]{1,0:T(8,128)(2,1)S(1)}, bf16[144,1536]{1,0:T(8,128)(2,1)S(1)}, u32[]{:S(2)}, u32[]{:S(2)}) collective-permute-start(bf16[144,1536]{1,0:T(8,128)(2,1)S(1)} %get-tuple-element.13), channel_id=1, source_target_pairs={{0,4},{2,6},{4,8},{5,1},{6,10},{7,3},{8,12},{9,5},{10,14},{11,7},{... | collective-permute-start | bytes 1327112 | tf_op jit(solution)/shard_map/ppermute | solution.py:400
  6.0 0.0 slice-start
  6.1 0.0 slice-start.2
  6.1 0.0 copy-start.7
  6.1 0.0 copy-start.3
  6.1 0.0 slice-start.1
  6.1 0.0 slice-start.3
  6.1 0.0 copy-start
  6.1 0.0 copy-start.1
  6.1 0.0 copy-start.2
  6.2 0.0 copy-start.4
  6.2 0.0 copy-start.5
  6.2 0.0 copy-start.6
  6.2 11.6 %all_to_all.10.desc_ref = s32[8,8,128]{2,1,0:T(8,128)S(1)} all-to-all(s32[8,8,128]{2,1,0:T(8,128)S(1)} %spread_list.1), channel_id=1, replica_groups=mesh['seq'=8,'rep'=4] {'seq'}, dimensions={0} | all-to-all | bytes 65536 | tf_op jit(solution)/shard_map/all_to_all | solution.py:404
  17.8 0.0 collective-permute-done.halo_ref
  17.8 0.0 collective-permute-start.1
  17.8 0.0 copy-done.7
  17.8 0.5 %collective-permute-start.2 = (bf16[1024]{0:T(1024)(128)(2,1)S(1)}, bf16[1024]{0:T(1024)(128)(2,1)S(1)}, u32[]{:S(2)}, u32[]{:S(2)}) collective-permute-start(bf16[1024]{0:T(1024)(128)(2,1)S(1)} %copy-done.7), channel_id=1, source_target_pairs={{0,1},{1,0},{2,3},{3,2},{4,5},{5,4},{6,7},{7,6},{8,9},{9,8},{10,11... | collective-permute-start | bytes 6152 | tf_op jit(solution)/shard_map/ppermute | solution.py:403
  18.3 0.0 copy-done.3
  18.3 1.0 %slot_table.1 = (s32[16,128]{1,0:T(8,128)S(1)}, s32[8,128]{1,0:T(8,128)S(1)}, bf16[400,1536]{1,0:T(8,128)(2,1)S(1)}) custom-call(s32[8,8,128]{2,1,0:T(8,128)S(1)} %all_to_all.10.desc_ref, bf16[256,1536]{1,0:T(8,128)(2,1)S(1)} %copy-done.3, bf16[144,1536]{1,0:T(8,128)(2,1)S(1)} %collective-permute-done.halo_ref), custom_call_target="tpu_custom_call" | custom-call | flops 491520000 | bytes 2000000 | tf_op jit(solution)/shard_map/slot_table/pallas_call | solution.py:97
  19.3 0.3 collective-permute-done.2.pair_bias_ref
  19.6 0.0 collective-permute-done.1.pair_ref
  19.6 0.0 collective-permute-done.3.pair_head_ref
  19.6 0.0 slice-done
  19.6 0.0 slice-done.2
  19.6 0.0 slice-done.1
  19.7 10.3 %trunk_and_head.1 = bf16[256,128]{1,0:T(8,128)(2,1)} custom-call(s32[16,128]{1,0:T(8,128)S(1)} %get-tuple-element.18.slots_ref, bf16[400,1536]{1,0:T(8,128)(2,1)S(1)} %get-tuple-element.19.early_ref, bf16[144,1536]{1,0:T(8,128)(2,1)S(1)} %collective-permute-done.1.pair_ref, bf16[4,1536]{1,0:T(4,128)(2,1)S(1)} %copy-done.4, bf16[1536]{0:T(1024)(128)(2,1)S(1)} %copy-done.5, ...), custom_call_target="tpu_custom_call" | custom-call | flops 6341787648 | bytes 29360128 | tf_op jit(solution)/shard_map/trunk_and_head/pallas_call | solution.py:278
  30.0 5.0 %all-to-all-start.1 = ((bf16[16,16,128]{2,1,0:T(8,128)(2,1)}), bf16[16,16,128]{2,1,0:T(8,128)(2,1)S(1)}, u32[]{:S(2)}, u32[]{:S(2)}) async-start(bf16[16,16,128]{2,1,0:T(8,128)(2,1)} %bitcast.2), calls=%async_computation.1 | async-start | bytes 131072 | tf_op jit(solution)/shard_map/all_to_all | solution.py:425
  35.0 6.8 %all-to-all-done.1 = bf16[16,16,128]{2,1,0:T(8,128)(2,1)S(1)} async-done(((bf16[16,16,128]{2,1,0:T(8,128)(2,1)}), bf16[16,16,128]{2,1,0:T(8,128)(2,1)S(1)}, u32[]{:S(2)}, u32[]{:S(2)}) %all-to-all-start.1) | async-done | bytes 65568 | tf_op jit(solution)/shard_map/all_to_all | solution.py:425
  41.7 1.2 %pick_scores.1 = f32[16,1024]{1,0:T(8,128)} custom-call(s32[128]{0:T(128)S(1)} %slice_bitcast_fusion.places_ref, bf16[256,128]{1,0:T(8,128)(2,1)S(1)} %bitcast.9), custom_call_target="tpu_custom_call" | custom-call | tf_op jit(solution)/shard_map/pick_scores/pallas_call | solution.py:434
  (11 shorter events, 0.0 us)
Async XLA Ops:
  1.1 18.5 %collective-permute-start.3 = (bf16[1536,1024]{1,0:T(8,128)(2,1)}, bf16[1536,1024]{1,0:T(8,128)(2,1)S(1)}, u32[]{:S(2)}, u32[]{:S(2)}) collective-permute-start(bf16[1536,1024]{1,0:T(8,128)(2,1)} %head_ref.1), channel_id=1, source_target_pairs={{0,1},{1,0},{2,3},{3,2},{4,5},{5,4},{6,7},{7,6},{8,9},{9,8},{10,11... | collective-permute-start | bytes 9437192 | tf_op jit(solution)/shard_map/ppermute | solution.py:402
  1.6 16.2 %collective-permute-start = (bf16[144,1536]{1,0:T(8,128)(2,1)S(1)}, bf16[144,1536]{1,0:T(8,128)(2,1)S(1)}, u32[]{:S(2)}, u32[]{:S(2)}) collective-permute-start(bf16[144,1536]{1,0:T(8,128)(2,1)S(1)} %get-tuple-element.13), channel_id=1, source_target_pairs={{0,4},{2,6},{4,8},{5,1},{6,10},{7,3},{8,12},{9,5},{10,14},{11,7},{... | collective-permute-start | bytes 1327112 | tf_op jit(solution)/shard_map/ppermute | solution.py:400
  6.0 13.6 %slice-start = ((s8[7077888]{0:T(1024)(128)(4,1)}), s8[4194304]{0:T(1024)(128)(4,1)S(1)}, s32[]{:S(2)}) async-start(s8[7077888]{0:T(1024)(128)(4,1)} %bitcast.5), calls=%async_computation.2 | async-start | bytes 8388608
  6.1 13.6 %slice-start.2 = ((s8[7077888]{0:T(1024)(128)(4,1)}), s8[4194304]{0:T(1024)(128)(4,1)S(1)}, s32[]{:S(2)}) async-start(s8[7077888]{0:T(1024)(128)(4,1)} %bitcast.7), calls=%async_computation.4 | async-start | bytes 8388608
  6.1 11.7 %copy-start.7 = (bf16[1024]{0:T(1024)(128)(2,1)S(1)}, bf16[1024]{0:T(1024)(128)(2,1)}, u32[]{:S(2)}) copy-start(bf16[1024]{0:T(1024)(128)(2,1)} %bias_ref.1) | copy-start | bytes 6148
  6.1 12.2 %copy-start.3 = (bf16[256,1536]{1,0:T(8,128)(2,1)S(1)}, bf16[256,1536]{1,0:T(8,128)(2,1)}, u32[]{:S(2)}) copy-start(bf16[256,1536]{1,0:T(8,128)(2,1)} %acts_ref.3) | copy-start | bytes 2359300
  6.1 13.5 %slice-start.1 = ((s8[7077888]{0:T(1024)(128)(4,1)}), s8[2883584]{0:T(1024)(128)(4,1)S(1)}, s32[]{:S(2)}) async-start(s8[7077888]{0:T(1024)(128)(4,1)} %bitcast.5), calls=%async_computation.3 | async-start | bytes 5767168
  6.1 13.5 %slice-start.3 = ((s8[7077888]{0:T(1024)(128)(4,1)}), s8[2883584]{0:T(1024)(128)(4,1)S(1)}, s32[]{:S(2)}) async-start(s8[7077888]{0:T(1024)(128)(4,1)} %bitcast.7), calls=%async_computation.5 | async-start | bytes 5767168
  6.1 13.5 %copy-start = (bf16[1536,1024]{1,0:T(8,128)(2,1)S(1)}, bf16[1536,1024]{1,0:T(8,128)(2,1)}, u32[]{:S(2)}) copy-start(bf16[1536,1024]{1,0:T(8,128)(2,1)} %head_ref.1) | copy-start | bytes 9437188
  6.1 13.5 %copy-start.1 = (bf16[768,1536]{1,0:T(8,128)(2,1)S(1)}, bf16[768,1536]{1,0:T(8,128)(2,1)}, u32[]{:S(2)}) copy-start(bf16[768,1536]{1,0:T(8,128)(2,1)} %proj1_ref.1) | copy-start | bytes 7077892
  6.1 13.5 %copy-start.2 = (bf16[768,1536]{1,0:T(8,128)(2,1)S(1)}, bf16[768,1536]{1,0:T(8,128)(2,1)}, u32[]{:S(2)}) copy-start(bf16[768,1536]{1,0:T(8,128)(2,1)} %proj2_ref.1) | copy-start | bytes 7077892
  6.2 13.5 %copy-start.4 = (bf16[4,1536]{1,0:T(4,128)(2,1)S(1)}, bf16[4,1536]{1,0:T(4,128)(2,1)}, u32[]{:S(2)}) copy-start(bf16[4,1536]{1,0:T(4,128)(2,1)} %delta_ref.1) | copy-start | bytes 36868
  6.2 13.5 %copy-start.5 = (bf16[1536]{0:T(1024)(128)(2,1)S(1)}, bf16[1536]{0:T(1024)(128)(2,1)}, u32[]{:S(2)}) copy-start(bf16[1536]{0:T(1024)(128)(2,1)} %gain1_ref.1) | copy-start | bytes 9220
  6.2 13.5 %copy-start.6 = (bf16[1536]{0:T(1024)(128)(2,1)S(1)}, bf16[1536]{0:T(1024)(128)(2,1)}, u32[]{:S(2)}) copy-start(bf16[1536]{0:T(1024)(128)(2,1)} %gain2_ref.1) | copy-start | bytes 9220
  17.8 1.8 %collective-permute-start.1 = (bf16[144,1536]{1,0:T(8,128)(2,1)S(1)}, bf16[144,1536]{1,0:T(8,128)(2,1)S(1)}, u32[]{:S(2)}, u32[]{:S(2)}) collective-permute-start(bf16[144,1536]{1,0:T(8,128)(2,1)S(1)} %collective-permute-done.halo_ref), channel_id=1, source_target_pairs={{0,1},{1,0},{2,3},{3,2},{4,5},{5,4},{6,7},{7,6},{8,9},{9,8},{10,11... | collective-permute-start | bytes 1327112 | tf_op jit(solution)/shard_map/ppermute | solution.py:406
  17.8 1.8 %collective-permute-start.2 = (bf16[1024]{0:T(1024)(128)(2,1)S(1)}, bf16[1024]{0:T(1024)(128)(2,1)S(1)}, u32[]{:S(2)}, u32[]{:S(2)}) collective-permute-start(bf16[1024]{0:T(1024)(128)(2,1)S(1)} %copy-done.7), channel_id=1, source_target_pairs={{0,1},{1,0},{2,3},{3,2},{4,5},{5,4},{6,7},{7,6},{8,9},{9,8},{10,11... | collective-permute-start | bytes 6152 | tf_op jit(solution)/shard_map/ppermute | solution.py:403
  30.0 11.8 %all-to-all-start.1 = ((bf16[16,16,128]{2,1,0:T(8,128)(2,1)}), bf16[16,16,128]{2,1,0:T(8,128)(2,1)S(1)}, u32[]{:S(2)}, u32[]{:S(2)}) async-start(bf16[16,16,128]{2,1,0:T(8,128)(2,1)} %bitcast.2), calls=%async_computation.1 | async-start | bytes 131072 | tf_op jit(solution)/shard_map/all_to_all | solution.py:425
